TPU v7x, 32 devices: a whole 2x2x4 slice. The times are simulated.
32 devices in a mesh: dp: 8 (over z, x), tensor: 4 (over y, core).
Axes of the slice: x: 2, y: 2, z: 4, core: 2. Of those that a mesh axis runs over, the one named last changes fastest.
Arguments:
- tokens: bfloat16 [4096, 1024], P(('dp', 'tensor')), may hold values from -6 to 6
- cotangent: bfloat16 [4096, 1024], P(('dp', 'tensor')), may hold values from -6 to 6
- norm1_gain: bfloat16 [1024], P('dp'), may hold values from 0.5 to 1.5
- w_query: bfloat16 [1024, 1024], P('dp', 'tensor'), may hold values from -0.1875 to 0.1875
- w_key: bfloat16 [1024, 1024], P('dp', 'tensor'), may hold values from -0.1875 to 0.1875
- w_value: bfloat16 [1024, 2048], P('dp', 'tensor'), may hold values from -0.1875 to 0.1875
- w_gate_out: bfloat16 [1024, 2048], P('dp', 'tensor'), may hold values from -0.1875 to 0.1875
- w_out: bfloat16 [1024, 2048], P('dp', 'tensor'), may hold values from -0.1875 to 0.1875
- w_beta: bfloat16 [1024, 8], P('dp', 'tensor'), may hold values from -0.1875 to 0.1875
- w_alpha: bfloat16 [1024, 8], P('dp', 'tensor'), may hold values from -0.1875 to 0.1875
- conv_query: bfloat16 [128, 8, 4], P('dp', 'tensor'), may hold values from -3 to 3
- conv_key: bfloat16 [128, 8, 4], P('dp', 'tensor'), may hold values from -3 to 3
- conv_value: bfloat16 [256, 8, 4], P('dp', 'tensor'), may hold values from -3 to 3
- a_log: bfloat16 [8], P('tensor'), may hold values from 0 to 2.765625
- dt_bias: bfloat16 [8], P('tensor'), may hold values from -6.875 to -2.296875
- head_gain: bfloat16 [256, 8], P('dp', 'tensor'), may hold values from 0.5 to 1.5
- norm2_gain: bfloat16 [1024], P('dp'), may hold values from 0.5 to 1.5
- w_up_gate: bfloat16 [1024, 2816], P('dp', 'tensor'), may hold values from -0.1875 to 0.1875
- w_up: bfloat16 [1024, 2816], P('dp', 'tensor'), may hold values from -0.1875 to 0.1875
- w_down: bfloat16 [1024, 2816], P('dp', 'tensor'), may hold values from -0.109375 to 0.109375
Outputs:
- out: bfloat16 [4096, 1024], P(('dp', 'tensor'))
- grad_tokens: float32 [4096, 1024], P(('dp', 'tensor'))
- grad_norm1_gain: float32 [1024], P('dp')
- grad_w_query: float32 [1024, 1024], P('dp', 'tensor')
- grad_w_key: float32 [1024, 1024], P('dp', 'tensor')
- grad_w_value: float32 [1024, 2048], P('dp', 'tensor')
- grad_w_gate_out: float32 [1024, 2048], P('dp', 'tensor')
- grad_w_out: float32 [1024, 2048], P('dp', 'tensor')
- grad_w_beta: float32 [1024, 8], P('dp', 'tensor')
- grad_w_alpha: float32 [1024, 8], P('dp', 'tensor')
- grad_conv_query: float32 [128, 8, 4], P('dp', 'tensor')
- grad_conv_key: float32 [128, 8, 4], P('dp', 'tensor')
- grad_conv_value: float32 [256, 8, 4], P('dp', 'tensor')
- grad_a_log: float32 [8], P('tensor')
- grad_dt_bias: float32 [8], P('tensor')
- grad_head_gain: float32 [256, 8], P('dp', 'tensor')
- grad_norm2_gain: float32 [1024], P('dp')
- grad_w_up_gate: float32 [1024, 2816], P('dp', 'tensor')
- grad_w_up: float32 [1024, 2816], P('dp', 'tensor')
- grad_w_down: float32 [1024, 2816], P('dp', 'tensor')
All inputs are finite; a program needn't handle non-finite values.
Results may differ from a plain program's by a relative error of at most 0.012.
Values may be sent and summed in bfloat16 or wider, within the bound.
A program may use at most 128 MiB of HBM per device.

v0:
```python
from functools import partial

import jax
import jax.numpy as jnp
from jax import lax
from jax.sharding import PartitionSpec as P

BLOCK = 64


epsilon = 1e-06
highest = lax.Precision.HIGHEST
contract_rows = (((0,), (0,)), ((), ()))
contract_cols = (((1,), (1,)), ((), ()))


def norm_forward(row_values):
    row_scale = lax.rsqrt(jnp.mean(row_values * row_values, axis=-1, keepdims=True) + epsilon)
    return (row_scale, row_values * row_scale)


def norm_backward(grad_normed, unit_values, row_scale, gain_values):
    grad_unit = grad_normed * gain_values
    return row_scale * (
        grad_unit - unit_values * jnp.mean(grad_unit * unit_values, axis=-1, keepdims=True)
    )


def short_conv(inputs, weights):
    tap_count = weights.shape[1]
    row_count = inputs.shape[0]
    padded = jnp.pad(inputs, ((tap_count - 1, 0), (0, 0)))
    result = jnp.zeros_like(inputs)
    for offset in range(tap_count):
        result = result + padded[offset : offset + row_count] * weights[:, offset]
    return result


def unit_length(values):
    return values * lax.rsqrt(jnp.sum(values * values, axis=-1, keepdims=True) + epsilon)


def split_heads(matrix_in, head_count):
    row_count, total_width = matrix_in.shape
    return jnp.swapaxes(matrix_in.reshape(row_count, head_count, total_width // head_count), 0, 1)


def channel_weights(conv_weights):
    key_dim, head_count, tap_count = conv_weights.shape
    return jnp.swapaxes(conv_weights, 0, 1).reshape(head_count * key_dim, tap_count)


def delta_rule(queries, keys_in, values, beta_rows, log_gates):
    head_count, seq_rows, key_dim = queries.shape
    value_dim = values.shape[2]
    block_count = seq_rows // BLOCK

    def blocked(matrix_in):
        return jnp.swapaxes(
            matrix_in.reshape((head_count, block_count, BLOCK) + matrix_in.shape[2:]), 0, 1
        )

    lower_incl = jnp.tril(jnp.ones((BLOCK, BLOCK), dtype=bool))
    lower_strict = jnp.tril(jnp.ones((BLOCK, BLOCK), dtype=bool), -1)
    identity_mat = jnp.eye(BLOCK, dtype=jnp.float32)
    solver = jax.vmap(partial(jax.scipy.linalg.solve_triangular, lower=True, unit_diagonal=True))

    def advance(carry_state, pieces):
        query_blk, key_blk, value_blk, beta_blk, gate_blk = pieces
        cum_decay = jnp.cumsum(gate_blk, axis=-1)
        differ = cum_decay[:, :, None] - cum_decay[:, None, :]
        decay_mat = jnp.where(lower_incl, jnp.exp(jnp.where(lower_incl, differ, 0.0)), 0.0)
        key_gram = jnp.einsum("hid,hjd->hij", key_blk, key_blk, precision=highest)
        system = identity_mat + jnp.where(
            lower_strict, key_gram * decay_mat * beta_blk[:, :, None], 0.0
        )
        right_side = jnp.concatenate(
            [
                key_blk * (beta_blk * jnp.exp(cum_decay))[:, :, None],
                value_blk * beta_blk[:, :, None],
            ],
            axis=-1,
        )
        solved = solver(system, right_side)
        key_part = solved[..., :key_dim]
        value_part = solved[..., key_dim:]
        fresh_values = value_part - jnp.einsum(
            "hcd,hde->hce", key_part, carry_state, precision=highest
        )
        scores = jnp.einsum("hid,hjd->hij", query_blk, key_blk, precision=highest) * decay_mat
        output_blk = jnp.einsum(
            "hcd,hde->hce",
            query_blk * jnp.exp(cum_decay)[:, :, None],
            carry_state,
            precision=highest,
        )
        output_blk = output_blk + jnp.einsum(
            "hij,hje->hie", scores, fresh_values, precision=highest
        )
        final_decay = cum_decay[:, -1]
        carried = jnp.exp(final_decay)[:, None, None] * carry_state
        carry_state = carried + jnp.einsum(
            "hcd,hce->hde",
            key_blk * jnp.exp(final_decay[:, None] - cum_decay)[:, :, None],
            fresh_values,
            precision=highest,
        )
        return (carry_state, output_blk)

    initial = jnp.zeros((head_count, key_dim, value_dim), jnp.float32)
    unused, outputs = lax.scan(
        advance,
        initial,
        (
            blocked(queries),
            blocked(keys_in),
            blocked(values),
            blocked(beta_rows),
            blocked(log_gates),
        ),
    )
    return jnp.swapaxes(outputs, 0, 1).reshape(head_count, seq_rows, value_dim)


def mixer_piece(
    proj_query,
    proj_key,
    proj_value,
    proj_gate,
    proj_beta,
    proj_alpha,
    conv_q_w,
    conv_k_w,
    conv_v_w,
    gain_heads,
    log_rate,
    rate_bias,
):
    head_count = proj_beta.shape[1]
    queries = split_heads(
        jax.nn.silu(short_conv(proj_query, channel_weights(conv_q_w))), head_count
    )
    queries = unit_length(queries) * queries.shape[2] ** (-0.5)
    keys_in = unit_length(
        split_heads(jax.nn.silu(short_conv(proj_key, channel_weights(conv_k_w))), head_count)
    )
    values = split_heads(jax.nn.silu(short_conv(proj_value, channel_weights(conv_v_w))), head_count)
    beta_rows = jax.nn.sigmoid(proj_beta).T
    log_gates = -jnp.exp(log_rate)[:, None] * jax.nn.softplus(proj_alpha + rate_bias).T
    mixed = delta_rule(queries, keys_in, values, beta_rows, log_gates)
    scaled = (
        mixed
        * lax.rsqrt(jnp.mean(mixed * mixed, axis=-1, keepdims=True) + epsilon)
        * gain_heads.T[:, None, :]
    )
    gated = scaled * split_heads(jax.nn.silu(proj_gate), head_count)
    return jnp.swapaxes(gated, 0, 1).reshape(gated.shape[1], -1)


def weight_grad(left_in, right_in):
    return lax.dot_general(left_in, right_in, contract_rows, preferred_element_type=jnp.float32)


def times_transpose(left_in, right_in):
    return lax.dot_general(left_in, right_in, contract_cols, preferred_element_type=jnp.float32)


def on_device(
    tokens,
    cotangent,
    norm1_gain,
    w_query,
    w_key,
    w_value,
    w_gate_out,
    w_out,
    w_beta,
    w_alpha,
    conv_query,
    conv_key,
    conv_value,
    a_log,
    dt_bias,
    head_gain,
    norm2_gain,
    w_up_gate,
    w_up,
    w_down,
):
    gathered = (
        lax.all_gather(norm1_gain, "dp", axis=0, tiled=True),
        lax.all_gather(w_query, "dp", axis=0, tiled=True),
        lax.all_gather(w_key, "dp", axis=0, tiled=True),
        lax.all_gather(w_value, "dp", axis=0, tiled=True),
        lax.all_gather(w_gate_out, "dp", axis=0, tiled=True),
        lax.all_gather(w_out, "dp", axis=0, tiled=True),
        lax.all_gather(w_beta, "dp", axis=0, tiled=True),
        lax.all_gather(w_alpha, "dp", axis=0, tiled=True),
        lax.all_gather(conv_query, "dp", axis=0, tiled=True),
        lax.all_gather(conv_key, "dp", axis=0, tiled=True),
        lax.all_gather(conv_value, "dp", axis=0, tiled=True),
        lax.all_gather(head_gain, "dp", axis=0, tiled=True),
    )
    gain_one = gathered[0].astype(jnp.float32)
    mixer_mats = (gathered[1], gathered[2], gathered[3], gathered[4], gathered[6], gathered[7])
    out_full = gathered[5]
    small_params = (
        gathered[8].astype(jnp.float32),
        gathered[9].astype(jnp.float32),
        gathered[10].astype(jnp.float32),
        gathered[11].astype(jnp.float32),
        a_log.astype(jnp.float32),
        dt_bias.astype(jnp.float32),
    )
    row_values = tokens.astype(jnp.float32)
    scale_one, unit_one = norm_forward(row_values)
    normed_local = (unit_one * gain_one).astype(jnp.bfloat16)
    normed_one = lax.all_gather(normed_local, "tensor", axis=0, tiled=True)
    projected = [
        jnp.dot(normed_one, weight, preferred_element_type=jnp.float32) for weight in mixer_mats
    ]
    mixed_full, pullback = jax.vjp(mixer_piece, *projected, *small_params)
    mixed = mixed_full.astype(jnp.bfloat16)
    middle = row_values + lax.psum_scatter(
        times_transpose(mixed, out_full), "tensor", scatter_dimension=0, tiled=True
    )
    ffn_full = (
        lax.all_gather(norm2_gain, "dp", axis=0, tiled=True),
        lax.all_gather(w_up_gate, "dp", axis=0, tiled=True),
        lax.all_gather(w_up, "dp", axis=0, tiled=True),
        lax.all_gather(w_down, "dp", axis=0, tiled=True),
    )
    gain_two = ffn_full[0].astype(jnp.float32)
    gate_full, up_full, down_full = (ffn_full[1], ffn_full[2], ffn_full[3])
    scale_two, unit_two = norm_forward(middle)
    normed_two = lax.all_gather(
        (unit_two * gain_two).astype(jnp.bfloat16), "tensor", axis=0, tiled=True
    )
    up_gate = jnp.dot(normed_two, gate_full, preferred_element_type=jnp.float32)
    up_lin = jnp.dot(normed_two, up_full, preferred_element_type=jnp.float32)
    hidden = (jax.nn.silu(up_gate) * up_lin).astype(jnp.bfloat16)
    result = (
        middle
        + lax.psum_scatter(
            times_transpose(hidden, down_full).astype(jnp.bfloat16),
            "tensor",
            scatter_dimension=0,
            tiled=True,
        ).astype(jnp.float32)
    ).astype(jnp.bfloat16)
    cot_full = lax.all_gather(cotangent, "tensor", axis=0, tiled=True)
    grad_hidden = jnp.dot(cot_full, down_full, preferred_element_type=jnp.float32)
    grad_down = weight_grad(cot_full, hidden)
    gate_sigmoid = jax.nn.sigmoid(up_gate)
    grad_gate = (
        grad_hidden * up_lin * gate_sigmoid * (1.0 + up_gate * (1.0 - gate_sigmoid))
    ).astype(jnp.bfloat16)
    grad_lin = (grad_hidden * up_gate * gate_sigmoid).astype(jnp.bfloat16)
    grad_up_gate = weight_grad(normed_two, grad_gate)
    grad_up = weight_grad(normed_two, grad_lin)
    grad_normed_two = lax.psum_scatter(
        times_transpose(grad_gate, gate_full) + times_transpose(grad_lin, up_full),
        "tensor",
        scatter_dimension=0,
        tiled=True,
    )
    grad_gain_two = jnp.sum(grad_normed_two * unit_two, axis=0)
    grad_middle = cotangent.astype(jnp.float32) + norm_backward(
        grad_normed_two, unit_two, scale_two, gain_two
    )
    mid_full = lax.all_gather(grad_middle.astype(jnp.bfloat16), "tensor", axis=0, tiled=True)
    grad_out_w = weight_grad(mid_full, mixed)
    grad_mixed = jnp.dot(mid_full, out_full, preferred_element_type=jnp.float32)
    pulled = pullback(grad_mixed)
    grad_proj = [grad_piece.astype(jnp.bfloat16) for grad_piece in pulled[:6]]
    grad_mats = [weight_grad(normed_one, grad_piece) for grad_piece in grad_proj]
    grad_normed_one = lax.psum_scatter(
        sum(
            (
                times_transpose(grad_piece, weight)
                for grad_piece, weight in zip(grad_proj, mixer_mats)
            )
        ).astype(jnp.bfloat16),
        "tensor",
        scatter_dimension=0,
        tiled=True,
    ).astype(jnp.float32)
    grad_gain_one = jnp.sum(grad_normed_one * unit_one, axis=0)
    grad_rows = grad_middle + norm_backward(grad_normed_one, unit_one, scale_one, gain_one)
    head_local = a_log.shape[0]
    head_total = head_local * lax.axis_size("tensor")
    head_start = lax.axis_index("tensor") * head_local

    def place_heads(local_grad):
        return lax.dynamic_update_slice(
            jnp.zeros((head_total,), jnp.float32), local_grad, (head_start,)
        )

    summed = lax.psum(
        (grad_gain_one, grad_gain_two, place_heads(pulled[10]), place_heads(pulled[11])),
        ("dp", "tensor"),
    )
    shard_rows = norm1_gain.shape[0]
    shard_start = lax.axis_index("dp") * shard_rows
    grad_gain_one_shard = lax.dynamic_slice_in_dim(summed[0], shard_start, shard_rows, 0)
    grad_gain_two_shard = lax.dynamic_slice_in_dim(summed[1], shard_start, shard_rows, 0)
    grad_rate = lax.dynamic_slice_in_dim(summed[2], head_start, head_local, 0)
    grad_rate_bias = lax.dynamic_slice_in_dim(summed[3], head_start, head_local, 0)
    every_sum = (
        lax.psum_scatter(grad_mats[0], "dp", scatter_dimension=0, tiled=True),
        lax.psum_scatter(grad_mats[1], "dp", scatter_dimension=0, tiled=True),
        lax.psum_scatter(grad_mats[2], "dp", scatter_dimension=0, tiled=True),
        lax.psum_scatter(grad_mats[3], "dp", scatter_dimension=0, tiled=True),
        lax.psum_scatter(grad_out_w, "dp", scatter_dimension=0, tiled=True),
        lax.psum_scatter(grad_mats[4], "dp", scatter_dimension=0, tiled=True),
        lax.psum_scatter(grad_mats[5], "dp", scatter_dimension=0, tiled=True),
        lax.psum_scatter(pulled[6], "dp", scatter_dimension=0, tiled=True),
        lax.psum_scatter(pulled[7], "dp", scatter_dimension=0, tiled=True),
        lax.psum_scatter(pulled[8], "dp", scatter_dimension=0, tiled=True),
        lax.psum_scatter(pulled[9], "dp", scatter_dimension=0, tiled=True),
        lax.psum_scatter(grad_up_gate, "dp", scatter_dimension=0, tiled=True),
        lax.psum_scatter(grad_up, "dp", scatter_dimension=0, tiled=True),
        lax.psum_scatter(grad_down, "dp", scatter_dimension=0, tiled=True),
    )
    mixer_sums = every_sum[:11]
    ffn_sums = every_sum[11:]
    return (
        result,
        grad_rows,
        grad_gain_one_shard,
        mixer_sums[0],
        mixer_sums[1],
        mixer_sums[2],
        mixer_sums[3],
        mixer_sums[4],
        mixer_sums[5],
        mixer_sums[6],
        mixer_sums[7],
        mixer_sums[8],
        mixer_sums[9],
        grad_rate,
        grad_rate_bias,
        mixer_sums[10],
        grad_gain_two_shard,
        ffn_sums[0],
        ffn_sums[1],
        ffn_sums[2],
    )


def solution(mesh):
    placed = (
        P(("dp", "tensor"), None),
        P(("dp", "tensor"), None),
        P("dp"),
        P("dp", "tensor"),
        P("dp", "tensor"),
        P("dp", "tensor"),
        P("dp", "tensor"),
        P("dp", "tensor"),
        P("dp", "tensor"),
        P("dp", "tensor"),
        P("dp", "tensor", None),
        P("dp", "tensor", None),
        P("dp", "tensor", None),
        P("tensor"),
        P("tensor"),
        P("dp", "tensor"),
        P("dp"),
        P("dp", "tensor"),
        P("dp", "tensor"),
        P("dp", "tensor"),
    )
    return jax.shard_map(
        on_device,
        mesh=mesh,
        in_specs=placed,
        out_specs=(
            P(("dp", "tensor"), None),
            P(("dp", "tensor"), None),
            P("dp"),
            P("dp", "tensor"),
            P("dp", "tensor"),
            P("dp", "tensor"),
            P("dp", "tensor"),
            P("dp", "tensor"),
            P("dp", "tensor"),
            P("dp", "tensor"),
            P("dp", "tensor", None),
            P("dp", "tensor", None),
            P("dp", "tensor", None),
            P("tensor"),
            P("tensor"),
            P("dp", "tensor"),
            P("dp"),
            P("dp", "tensor"),
            P("dp", "tensor"),
            P("dp", "tensor"),
        ),
        check_vma=False,
    )
```

profile of v0, /device:TPU:0, one launch (start us, length us, event | category | flops | bytes accessed | tf_op | source)
XLA Modules:
  0.0 2057.6 jit_solution(4061376049928933037)
XLA Ops:
  35.0 31.9 %all_gather.63 = bf16[1024,256]{1,0:T(8,128)(2,1)S(1)} all-gather(bf16[128,256]{1,0:T(8,128)(2,1)} %param.28), channel_id=1, replica_groups=mesh['dp'=8,'tensor'=4] {'dp'}, dimensions={0}, use_global_device_ids=true | all-gather | bytes 589824 | tf_op jit(solution)/shard_map/all_gather | solution.py:193
  67.0 30.8 %all_gather.64 = bf16[128,2,4]{2,1,0:T(2,128)(2,1)S(1)} all-gather(bf16[16,2,4]{2,1,0:T(2,128)(2,1)S(1)} %copy.188), channel_id=1, replica_groups=mesh['dp'=8,'tensor'=4] {'dp'}, dimensions={0}, use_global_device_ids=true | all-gather | bytes 2304 | tf_op jit(solution)/shard_map/all_gather | solution.py:200
  98.0 34.1 %all_gather.68 = bf16[1024,256]{1,0:T(8,128)(2,1)} all-gather(bf16[128,256]{1,0:T(8,128)(2,1)S(1)} %copy-done.39), channel_id=1, replica_groups=mesh['dp'=8,'tensor'=4] {'dp'}, dimensions={0}, use_global_device_ids=true | all-gather | bytes 589824 | tf_op jit(solution)/shard_map/all_gather | solution.py:192
  132.2 30.7 %all_gather.69 = bf16[128,2,4]{2,1,0:T(2,128)(2,1)S(1)} all-gather(bf16[16,2,4]{2,1,0:T(2,128)(2,1)S(1)} %copy.195), channel_id=1, replica_groups=mesh['dp'=8,'tensor'=4] {'dp'}, dimensions={0}, use_global_device_ids=true | all-gather | bytes 2304 | tf_op jit(solution)/shard_map/all_gather | solution.py:199
  197.9 30.5 %all_gather.67 = bf16[256,2,4]{2,1,0:T(2,128)(2,1)S(1)} all-gather(bf16[32,2,4]{2,1,0:T(2,128)(2,1)S(1)} %copy.192), channel_id=1, replica_groups=mesh['dp'=8,'tensor'=4] {'dp'}, dimensions={0}, use_global_device_ids=true | all-gather | bytes 4608 | tf_op jit(solution)/shard_map/all_gather | solution.py:201
  258.3 186.0 %while.90 = (s32[]{:T(128)}, f32[2,128,256]{2,1,0:T(8,128)S(1)}, f32[8,2,64,256]{3,2,0,1:T(8,128)S(1)}, f32[8,2,64,64]{3,2,1,0:T(8,128)}, f32[8,2,64,64]{3,2,1,0...) while((s32[]{:T(128)}, f32[2,128,256]{2,1,0:T(8,128)S(1)}, ...), condition=%wide.region_5.6_spmd.clone.clone, body=%wide.region_3.5_spmd.clone.clone.sunk | while | flops 239923776 | bytes 5326754 | solution.py:111
  488.8 40.5 %all-gather.24.cloned.1.call-done = bf16[1024,704]{0,1:T(8,128)(2,1)} async-done(((bf16[128,704]{0,1:T(8,128)(2,1)}), bf16[1024,704]{0,1:T(8,128)(2,1)}) %all-gather.24.cloned.1.call-update) | async-done | bytes 1441808 | tf_op jit(solution)/shard_map/all_gather | solution.py:229
  550.1 41.3 %all-gather.26.cloned.1.call-done = bf16[1024,704]{0,1:T(8,128)(2,1)} async-done(((bf16[128,704]{0,1:T(8,128)(2,1)}), bf16[1024,704]{0,1:T(8,128)(2,1)}) %all-gather.26.cloned.1.call-update) | async-done | bytes 1441808 | tf_op jit(solution)/shard_map/all_gather | solution.py:230
  607.9 44.9 %all-gather.28.cloned.1.call-done = bf16[1024,704]{0,1:T(8,128)(2,1)} async-done(((bf16[128,704]{0,1:T(8,128)(2,1)}), bf16[1024,704]{0,1:T(8,128)(2,1)}) %all-gather.28.cloned.1.call-update) | async-done | bytes 1441808 | tf_op jit(solution)/shard_map/all_gather | solution.py:231
  725.4 290.9 %while.91 = (s32[]{:T(128)}, f32[2,128,256]{2,1,0:T(8,128)S(1)}, f32[8,2,64,128]{3,2,0,1:T(8,128)}, f32[8,2,64,128]{3,2,0,1:T(8,128)}, f32[8,2,64,256]{3,2,0,1:T...) while((s32[]{:T(128)}, f32[2,128,256]{2,1,0:T(8,128)S(1)}, ...), condition=%wide.region_24.25_spmd.clone.clone, body=%wide.region_13.24_spmd.clone.clone.sunk | while | flops 485758016 | bytes 8084536 | solution.py:111
  1096.0 63.4 %reduce-scatter.61.cloned.1.call-done = f32[16,8]{1,0:T(8,128)} async-done(((f32[128,8]{1,0:T(8,128)}), f32[16,8]{1,0:T(8,128)}) %reduce-scatter.61.cloned.1.call-update) | async-done | bytes 528
  1160.7 63.4 %reduce-scatter.59.cloned.1.call-done = f32[16,8]{1,0:T(8,128)} async-done(((f32[128,8]{1,0:T(8,128)}), f32[16,8]{1,0:T(8,128)}) %reduce-scatter.59.cloned.1.call-update) | async-done | bytes 528
  1225.5 63.4 %reduce-scatter.63.cloned.1.call-done = f32[32,8]{1,0:T(8,128)} async-done(((f32[256,8]{1,0:T(8,128)}), f32[32,8]{1,0:T(8,128)}) %reduce-scatter.63.cloned.1.call-update) | async-done | bytes 1040
  1290.2 63.5 %reduce-scatter.57.cloned.1.call-done = f32[128,2]{1,0:T(8,128)} async-done(((f32[1024,2]{1,0:T(8,128)}), f32[128,2]{1,0:T(8,128)}) %reduce-scatter.57.cloned.1.call-update) | async-done | bytes 1040
  1355.2 64.0 %reduce-scatter.55.cloned.1.call-done = f32[128,2]{1,0:T(8,128)} async-done(((f32[1024,2]{1,0:T(8,128)}), f32[128,2]{1,0:T(8,128)}) %reduce-scatter.55.cloned.1.call-update) | async-done | bytes 1040
  1446.7 39.5 %all-reduce.30 = (f32[1024]{0:T(1024)S(1)}, f32[8]{0:T(128)S(1)}, f32[8]{0:T(128)S(1)}, f32[1024]{0:T(1024)S(1)}) all-reduce(f32[1024]{0:T(1024)S(1)} %get-tuple-element.2122, f32[8]{0:T(128)S(1)} %multiply_dynamic-update-slice_fusion.2, f32[8]{0:T(128)S(1)} %dynamic_update_slice.236, ...), channel_id=1, replica_groups=mesh['dp'=8,'tensor'=4] {'dp','tensor'}, use_global_device_ids=true, to_apply=%region_30.31 | all-reduce | flops 2064 | bytes 16512 | tf_op jit(solution)/shard_map/psum | solution.py:299
  1490.7 58.9 %reduce-scatter.49.cloned.1.call-done = f32[128,704]{0,1:T(8,128)} async-done(((f32[1024,704]{0,1:T(8,128)}), f32[128,704]{0,1:T(8,128)}) %reduce-scatter.49.cloned.1.call-update) | async-done | bytes 360464 | tf_op jit(solution)/shard_map/reduce_scatter | solution.py:321
  1549.7 76.2 %reduce-scatter.51.cloned.1.call-done = f32[128,704]{0,1:T(8,128)} async-done(((f32[1024,704]{0,1:T(8,128)}), f32[128,704]{0,1:T(8,128)}) %reduce-scatter.51.cloned.1.call-update) | async-done | bytes 360464 | tf_op jit(solution)/shard_map/reduce_scatter | solution.py:322
  1625.9 76.2 %reduce-scatter.53.cloned.1.call-done = f32[128,704]{0,1:T(8,128)} async-done(((f32[1024,704]{0,1:T(8,128)}), f32[128,704]{0,1:T(8,128)}) %reduce-scatter.53.cloned.1.call-update) | async-done | bytes 360464 | tf_op jit(solution)/shard_map/reduce_scatter | solution.py:323
  1702.1 67.3 %reduce-scatter.41.cloned.1.call-done = f32[128,256]{1,0:T(8,128)} async-done(((f32[1024,256]{1,0:T(8,128)}), f32[128,256]{1,0:T(8,128)}) %reduce-scatter.41.cloned.1.call-update) | async-done | bytes 131088 | tf_op jit(solution)/shard_map/reduce_scatter | solution.py:311
  1769.3 67.2 %reduce-scatter.39.cloned.1.call-done = f32[128,256]{1,0:T(8,128)} async-done(((f32[1024,256]{1,0:T(8,128)}), f32[128,256]{1,0:T(8,128)}) %reduce-scatter.39.cloned.1.call-update) | async-done | bytes 131088 | tf_op jit(solution)/shard_map/reduce_scatter | solution.py:310
  1836.5 71.2 %reduce-scatter.47.cloned.1.call-done = f32[128,512]{1,0:T(8,128)} async-done(((f32[1024,512]{1,0:T(8,128)}), f32[128,512]{1,0:T(8,128)}) %reduce-scatter.47.cloned.1.call-update) | async-done | bytes 262160 | tf_op jit(solution)/shard_map/reduce_scatter | solution.py:314
  1907.7 71.3 %reduce-scatter.43.cloned.1.call-done = f32[128,512]{1,0:T(8,128)} async-done(((f32[1024,512]{1,0:T(8,128)}), f32[128,512]{1,0:T(8,128)}) %reduce-scatter.43.cloned.1.call-update) | async-done | bytes 262160 | tf_op jit(solution)/shard_map/reduce_scatter | solution.py:312
  1979.0 71.6 %reduce-scatter.45.cloned.1.call-done = f32[128,512]{1,0:T(8,128)} async-done(((f32[1024,512]{1,0:T(8,128)}), f32[128,512]{1,0:T(8,128)}) %reduce-scatter.45.cloned.1.call-update) | async-done | bytes 262160 | tf_op jit(solution)/shard_map/reduce_scatter | solution.py:313
  (874 shorter events, 838.6 us)
Async XLA Ops:
  7.2 237.9 %all-gather.14.cloned.1.call-start = ((), (), s32[]{:S(2)}) async-start(), calls=%async_computation.18 | async-start | bytes 1310720 | tf_op jit(solution)/shard_map/all_gather | solution.py:218
  32.7 220.8 %all-gather.16.cloned.1.call-start = ((), (), s32[]{:S(2)}) async-start(), calls=%async_computation.19 | async-start | bytes 1179648 | tf_op jit(solution)/shard_map/all_gather | solution.py:194
  33.5 411.1 %all-gather.18.cloned.1.call-start = ((), (), s32[]{:S(2)}) async-start(), calls=%async_computation.20 | async-start | bytes 1179648 | tf_op jit(solution)/shard_map/all_gather | solution.py:195
  34.2 416.7 %all-gather.20.cloned.1.call-start = ((), (), s32[]{:S(2)}) async-start(), calls=%async_computation.21 | async-start | bytes 1179648 | tf_op jit(solution)/shard_map/all_gather | solution.py:196
  34.8 449.6 %reduce-scatter.31.cloned.1.call-start = ((), (), s32[]{:S(2)}) async-start(), calls=%async_computation.22 | async-start | bytes 2621440 | tf_op jit(solution)/shard_map/reduce_scatter | solution.py:224
  487.2 120.7 %all-gather.30.cloned.1.call-start = ((), (), s32[]{:S(2)}) async-start(), calls=%async_computation.28 | async-start | bytes 1310720 | tf_op jit(solution)/shard_map/all_gather | solution.py:251
  487.9 164.9 %all-gather.28.cloned.1.call-start = ((), (), s32[]{:S(2)}) async-start(), calls=%async_computation.26 | async-start | bytes 1622016 | tf_op jit(solution)/shard_map/all_gather | solution.py:231
  488.5 203.0 %reduce-scatter.35.cloned.1.call-start = ((), (), s32[]{:S(2)}) async-start(), calls=%async_computation.29 | async-start | bytes 2621440 | tf_op jit(solution)/shard_map/reduce_scatter | solution.py:261
  694.8 399.8 %reduce-scatter.65.cloned.1.call-start = ((), (), s32[]{:S(2)}) async-start(), calls=%async_computation.45 | async-start | bytes 147456
  1032.6 126.8 %reduce-scatter.61.cloned.1.call-start = ((), (), s32[]{:S(2)}) async-start(), calls=%async_computation.43 | async-start | bytes 73728
  1033.4 190.7 %reduce-scatter.59.cloned.1.call-start = ((), (), s32[]{:S(2)}) async-start(), calls=%async_computation.42 | async-start | bytes 73728
  1034.2 254.7 %reduce-scatter.63.cloned.1.call-start = ((), (), s32[]{:S(2)}) async-start(), calls=%async_computation.44 | async-start | bytes 147456
  1045.2 308.5 %reduce-scatter.57.cloned.1.call-start = ((), (), s32[]{:S(2)}) async-start(), calls=%async_computation.41 | async-start | bytes 589824
  1048.8 370.4 %reduce-scatter.55.cloned.1.call-start = ((), (), s32[]{:S(2)}) async-start(), calls=%async_computation.40 | async-start | bytes 589824
  1050.1 395.3 %reduce-scatter.37.cloned.1.call-start = ((), (), s32[]{:S(2)}) async-start(), calls=%async_computation.31 | async-start | bytes 1310720 | tf_op jit(solution)/shard_map/reduce_scatter | solution.py:277
  1057.9 430.6 %reduce-scatter.33.cloned.1.call-start = ((), (), s32[]{:S(2)}) async-start(), calls=%async_computation.27 | async-start | bytes 1310720 | tf_op jit(solution)/shard_map/reduce_scatter | solution.py:244
  1061.6 488.1 %reduce-scatter.49.cloned.1.call-start = ((), (), s32[]{:S(2)}) async-start(), calls=%async_computation.37 | async-start | bytes 3244032 | tf_op jit(solution)/shard_map/reduce_scatter | solution.py:321
  1065.6 560.3 %reduce-scatter.51.cloned.1.call-start = ((), (), s32[]{:S(2)}) async-start(), calls=%async_computation.38 | async-start | bytes 3244032 | tf_op jit(solution)/shard_map/reduce_scatter | solution.py:322
  1069.6 632.4 %reduce-scatter.53.cloned.1.call-start = ((), (), s32[]{:S(2)}) async-start(), calls=%async_computation.39 | async-start | bytes 3244032 | tf_op jit(solution)/shard_map/reduce_scatter | solution.py:323
  1073.7 695.6 %reduce-scatter.41.cloned.1.call-start = ((), (), s32[]{:S(2)}) async-start(), calls=%async_computation.33 | async-start | bytes 1179648 | tf_op jit(solution)/shard_map/reduce_scatter | solution.py:311
  1075.2 761.3 %reduce-scatter.39.cloned.1.call-start = ((), (), s32[]{:S(2)}) async-start(), calls=%async_computation.32 | async-start | bytes 1179648 | tf_op jit(solution)/shard_map/reduce_scatter | solution.py:310
  1077.8 829.9 %reduce-scatter.47.cloned.1.call-start = ((), (), s32[]{:S(2)}) async-start(), calls=%async_computation.36 | async-start | bytes 2359296 | tf_op jit(solution)/shard_map/reduce_scatter | solution.py:314
  1081.2 897.8 %reduce-scatter.43.cloned.1.call-start = ((), (), s32[]{:S(2)}) async-start(), calls=%async_computation.34 | async-start | bytes 2359296 | tf_op jit(solution)/shard_map/reduce_scatter | solution.py:312
  1083.4 967.2 %reduce-scatter.45.cloned.1.call-start = ((), (), s32[]{:S(2)}) async-start(), calls=%async_computation.35 | async-start | bytes 2359296 | tf_op jit(solution)/shard_map/reduce_scatter | solution.py:313
  (68 other events, 4719.2 us)
Sparse Core Ops, SparseCore 0:
  49.0 41.2 all-gather.15
  92.4 40.7 all-gather.17
  135.2 39.3 all-gather.19
  454.5 29.8 reduce-scatter.30
  486.3 42.9 all-gather.23
  548.4 42.9 all-gather.25
  609.8 42.9 all-gather.27
  662.2 29.3 reduce-scatter.34
  1032.7 61.8 reduce-scatter.64
  1097.9 61.4 reduce-scatter.60
  1162.6 61.4 reduce-scatter.58
  1227.9 60.9 reduce-scatter.62
  1292.0 61.6 reduce-scatter.56
  1357.5 61.6 reduce-scatter.54
  1421.7 23.7 reduce-scatter.36
  1447.8 24.7 reduce-scatter.32
  1476.8 72.8 reduce-scatter.48
  1553.8 72.0 reduce-scatter.50
  1630.0 71.9 reduce-scatter.52
  1705.9 63.3 reduce-scatter.40
  1773.3 63.1 reduce-scatter.38
  1840.5 67.1 reduce-scatter.46
  1911.7 67.3 reduce-scatter.42
  1983.1 67.4 reduce-scatter.44
  (4 shorter events, 60.2 us)
where the time goes:
time: 2070 us; the launch traced here: 2060 us
  waiting for transfers between devices  1130 us (55%)
  blocking collectives  289 us (14%)
  other arithmetic  270 us (13%)
  matrix products  262 us (13%)
  local copies, waits for them, and re-layouts  79.8 us (4%)
    unnamed x34, waiting for transfers between devices  331 us
    another operation x80, other arithmetic, advance(): solved = solver(system, right_side)  166 us
    reduce_scatter x1, waiting for transfers between devices, on_device(): lax.psum_scatter(grad_up, 'dp', scatter_dimension=0, tiled=True)  76.2 us
    reduce_scatter x1, waiting for transfers between devices, on_device(): lax.psum_scatter(grad_down, 'dp', scatter_dimension=0, tiled=True)  76.2 us
    reduce_scatter x1, waiting for transfers between devices, on_device(): lax.psum_scatter(grad_mats[3], 'dp', scatter_dimension=0, tiled=True)  71.6 us
    reduce_scatter x1, waiting for transfers between devices, on_device(): lax.psum_scatter(grad_mats[2], 'dp', scatter_dimension=0, tiled=True)  71.3 us
    reduce_scatter x1, waiting for transfers between devices, on_device(): lax.psum_scatter(grad_out_w, 'dp', scatter_dimension=0, tiled=True)  71.2 us
    reduce_scatter x1, waiting for transfers between devices, on_device(): lax.psum_scatter(grad_mats[1], 'dp', scatter_dimension=0, tiled=True)  67.3 us
  transfers between devices with their start and end apart: 28, of which 23 were waited for; matrix products, arithmetic and copies ran while one was open for 13% of the time, Pallas kernels for 0%

commit v1 on v0

v1 whole, which is shorter than its diff:
```python
import jax
import jax.numpy as jnp
from jax import lax
from jax.experimental import pallas as pl
from jax.experimental.pallas import tpu as pltpu
from jax.sharding import PartitionSpec as P

epsilon = 1e-06
CHUNK = 128
LANES = 128
contract_rows = (((0,), (0,)), ((), ()))
contract_cols = (((1,), (1,)), ((), ()))
contract_plain = (((1,), (0,)), ((), ()))
highest = lax.Precision.HIGHEST


def norm_forward(row_values):
    row_scale = lax.rsqrt(jnp.mean(row_values * row_values, axis=-1, keepdims=True) + epsilon)
    return (row_scale, row_values * row_scale)


def norm_backward(grad_normed, unit_values, row_scale, gain_values):
    grad_unit = grad_normed * gain_values
    return row_scale * (
        grad_unit - unit_values * jnp.mean(grad_unit * unit_values, axis=-1, keepdims=True)
    )


def weight_grad(left_in, right_in):
    return lax.dot_general(left_in, right_in, contract_rows, preferred_element_type=jnp.float32)


def times_transpose(left_in, right_in):
    return lax.dot_general(left_in, right_in, contract_cols, preferred_element_type=jnp.float32)


def exact_dot(left_in, right_in, dims=contract_plain):
    return lax.dot_general(
        left_in, right_in, dims, precision=highest, preferred_element_type=jnp.float32
    )


def silu(values):
    return values * lax.logistic(values)


def unit_length(values):
    return values * lax.rsqrt(jnp.sum(values * values, axis=-1, keepdims=True) + epsilon)


def triangle_masks(size):
    row = lax.broadcasted_iota(jnp.int32, (size, size), 0)
    col = lax.broadcasted_iota(jnp.int32, (size, size), 1)
    return row, col


def unit_lower_inverse(lower):
    size = lower.shape[0]
    row, col = triangle_masks(size)
    inverse = jnp.where(row == col, 1.0, 0.0)
    bit = 0
    while (1 << bit) < size:
        joined = ((row >> (bit + 1)) == (col >> (bit + 1))) & ((row >> bit) != (col >> bit))
        part = jnp.where(joined, lower, 0.0)
        if bit == 0:
            inverse = inverse - part
        else:
            inverse = inverse - exact_dot(inverse, exact_dot(part, inverse))
        bit += 1
    return inverse


@jax.custom_vjp
def known_inverse(lower, inverse):
    return inverse


def known_inverse_fwd(lower, inverse):
    return inverse, inverse


def known_inverse_bwd(inverse, grad):
    turned = inverse.T
    return -exact_dot(exact_dot(turned, grad), turned), jnp.zeros_like(inverse)


known_inverse.defvjp(known_inverse_fwd, known_inverse_bwd)


def mixer_chunk(conv_q, conv_k, conv_v, proj_gate, beta, gate, gain, state, inverter):
    size, key_dim = conv_q.shape
    row, col = triangle_masks(size)
    strict = row > col
    lower = row >= col
    query = unit_length(silu(conv_q)) * key_dim ** (-0.5)
    key = unit_length(silu(conv_k))
    value = silu(conv_v)
    wide = jnp.broadcast_to(gate, (size, size))
    decay_col = jnp.sum(jnp.where(lower, wide.T, 0.0), axis=1, keepdims=True)
    decay_row = jnp.sum(jnp.where(row <= col, wide, 0.0), axis=0, keepdims=True)
    decay_end = jnp.sum(gate, axis=0, keepdims=True)
    differ = jnp.where(strict, decay_col - decay_row, 0.0)
    decay = jnp.where(lower, jnp.exp(differ), 0.0)
    system = jnp.where(strict, exact_dot(key, key, contract_cols) * decay * beta, 0.0)
    inverse = inverter(system)
    grown = jnp.exp(decay_col)
    fresh = exact_dot(inverse, value * beta - exact_dot(key * (beta * grown), state))
    scores = exact_dot(query, key, contract_cols) * decay
    mixed = exact_dot(query * grown, state) + exact_dot(scores, fresh)
    new_state = jnp.exp(decay_end) * state + exact_dot(
        key * jnp.exp(decay_end - decay_col), fresh, contract_rows
    )
    scaled = mixed * lax.rsqrt(jnp.mean(mixed * mixed, axis=-1, keepdims=True) + epsilon) * gain
    return scaled * silu(proj_gate), new_state, inverse


def head_slices(head, heads, key_dim, value_dim):
    q_at = head * key_dim
    k_at = (heads + head) * key_dim
    v_at = 2 * heads * key_dim + head * value_dim
    return (
        slice(q_at, q_at + key_dim),
        slice(k_at, k_at + key_dim),
        slice(v_at, v_at + value_dim),
        slice(head * value_dim, (head + 1) * value_dim),
    )


def mixer_forward_kernel(
    heads, key_dim, value_dim, conv_ref, pgate_ref, rates_ref, gain_ref,
    gated_ref, states_ref, inverses_ref, state_ref,
):
    @pl.when(pl.program_id(0) == 0)
    def _():
        state_ref[...] = jnp.zeros_like(state_ref)

    for head in range(heads):
        at_q, at_k, at_v, at_g = head_slices(head, heads, key_dim, value_dim)
        state = state_ref[head]
        gated, new_state, inverse = mixer_chunk(
            conv_ref[:, at_q],
            conv_ref[:, at_k],
            conv_ref[:, at_v],
            pgate_ref[:, at_g],
            rates_ref[:, head : head + 1],
            rates_ref[:, heads + head : heads + head + 1],
            gain_ref[:, at_g],
            state,
            unit_lower_inverse,
        )
        gated_ref[:, at_g] = gated.astype(gated_ref.dtype)
        states_ref[0, head] = state
        inverses_ref[0, head] = inverse
        state_ref[head] = new_state


def mixer_backward_kernel(
    heads, key_dim, value_dim, conv_ref, pgate_ref, rates_ref, gain_ref, states_ref,
    inverses_ref, grad_ref, gconv_ref, gpgate_ref, grates_ref, ggain_ref, gstate_ref,
):
    @pl.when(pl.program_id(0) == 0)
    def _():
        gstate_ref[...] = jnp.zeros_like(gstate_ref)
        ggain_ref[...] = jnp.zeros_like(ggain_ref)

    lane = lax.broadcasted_iota(jnp.int32, grates_ref.shape, 1)
    rates_grad = jnp.zeros(grates_ref.shape, jnp.float32)
    for head in range(heads):
        at_q, at_k, at_v, at_g = head_slices(head, heads, key_dim, value_dim)
        inverse = inverses_ref[0, head]

        def run(*operands):
            gated, new_state, _ = mixer_chunk(
                *operands, lambda system: known_inverse(system, inverse)
            )
            return gated, new_state

        _, pull = jax.vjp(
            run,
            conv_ref[:, at_q],
            conv_ref[:, at_k],
            conv_ref[:, at_v],
            pgate_ref[:, at_g],
            rates_ref[:, head : head + 1],
            rates_ref[:, heads + head : heads + head + 1],
            gain_ref[:, at_g],
            states_ref[0, head],
        )
        pulled = pull((grad_ref[:, at_g], gstate_ref[head]))
        gconv_ref[:, at_q] = pulled[0]
        gconv_ref[:, at_k] = pulled[1]
        gconv_ref[:, at_v] = pulled[2]
        gpgate_ref[:, at_g] = pulled[3]
        rates_grad = jnp.where(lane == head, pulled[4], rates_grad)
        rates_grad = jnp.where(lane == heads + head, pulled[5], rates_grad)
        ggain_ref[:, at_g] += pulled[6]
        gstate_ref[head] = pulled[7]
    grates_ref[...] = rates_grad


def row_block(width, order):
    return pl.BlockSpec((CHUNK, width), lambda step: (order(step), 0))


def mixer_forward(conv_all, proj_gate, rates, gain_row, heads, key_dim, value_dim):
    rows, conv_width = conv_all.shape
    steps = rows // CHUNK
    forward = lambda step: step
    width = heads * value_dim
    return pl.pallas_call(
        lambda *refs: mixer_forward_kernel(heads, key_dim, value_dim, *refs),
        name="mixer_forward",
        grid=(steps,),
        in_specs=[
            row_block(conv_width, forward),
            row_block(width, forward),
            row_block(rates.shape[1], forward),
            pl.BlockSpec((1, width), lambda step: (0, 0)),
        ],
        out_specs=[
            row_block(width, forward),
            pl.BlockSpec((1, heads, key_dim, value_dim), lambda step: (step, 0, 0, 0)),
            pl.BlockSpec((1, heads, CHUNK, CHUNK), lambda step: (step, 0, 0, 0)),
        ],
        out_shape=[
            jax.ShapeDtypeStruct((rows, width), jnp.bfloat16),
            jax.ShapeDtypeStruct((steps, heads, key_dim, value_dim), jnp.float32),
            jax.ShapeDtypeStruct((steps, heads, CHUNK, CHUNK), jnp.float32),
        ],
        scratch_shapes=[pltpu.VMEM((heads, key_dim, value_dim), jnp.float32)],
        cost_estimate=pl.CostEstimate(
            flops=80_000_000_00, bytes_accessed=8_000_000, transcendentals=1_000_000
        ),
    )(conv_all, proj_gate, rates, gain_row)


def mixer_backward(
    conv_all, proj_gate, rates, gain_row, states, inverses, grad_gated, heads, key_dim, value_dim
):
    rows, conv_width = conv_all.shape
    steps = rows // CHUNK
    back = lambda step: steps - 1 - step
    width = heads * value_dim
    return pl.pallas_call(
        lambda *refs: mixer_backward_kernel(heads, key_dim, value_dim, *refs),
        name="mixer_backward",
        grid=(steps,),
        in_specs=[
            row_block(conv_width, back),
            row_block(width, back),
            row_block(rates.shape[1], back),
            pl.BlockSpec((1, width), lambda step: (0, 0)),
            pl.BlockSpec((1, heads, key_dim, value_dim), lambda step: (back(step), 0, 0, 0)),
            pl.BlockSpec((1, heads, CHUNK, CHUNK), lambda step: (back(step), 0, 0, 0)),
            row_block(width, back),
        ],
        out_specs=[
            row_block(conv_width, back),
            row_block(width, back),
            row_block(rates.shape[1], back),
            pl.BlockSpec((1, width), lambda step: (0, 0)),
        ],
        out_shape=[
            jax.ShapeDtypeStruct((rows, conv_width), jnp.float32),
            jax.ShapeDtypeStruct((rows, width), jnp.float32),
            jax.ShapeDtypeStruct(rates.shape, jnp.float32),
            jax.ShapeDtypeStruct((1, width), jnp.float32),
        ],
        scratch_shapes=[pltpu.VMEM((heads, key_dim, value_dim), jnp.float32)],
        cost_estimate=pl.CostEstimate(
            flops=200_000_000_00, bytes_accessed=12_000_000, transcendentals=2_000_000
        ),
    )(conv_all, proj_gate, rates, gain_row, states, inverses, grad_gated)


def short_conv(inputs, weights):
    tap_count = weights.shape[1]
    row_count = inputs.shape[0]
    padded = jnp.pad(inputs, ((tap_count - 1, 0), (0, 0)))
    result = jnp.zeros_like(inputs)
    for offset in range(tap_count):
        result = result + padded[offset : offset + row_count] * weights[:, offset]
    return result


def channel_weights(conv_weights):
    key_dim, head_count, tap_count = conv_weights.shape
    return jnp.swapaxes(conv_weights, 0, 1).reshape(head_count * key_dim, tap_count)


def pad_columns(matrix_in, width):
    return jnp.pad(matrix_in, ((0, 0), (0, width - matrix_in.shape[1])))


def round_up(size, step):
    return -(-size // step) * step


def as_columns(values, rows):
    flat = values.reshape(-1)
    return jnp.pad(flat, (0, round_up(flat.shape[0], rows) - flat.shape[0])).reshape(rows, -1)


def rate_terms(proj_beta, proj_alpha, log_rate, rate_bias):
    log_gates = -jnp.exp(log_rate) * jax.nn.softplus(proj_alpha + rate_bias)
    return jnp.concatenate([jax.nn.sigmoid(proj_beta), log_gates], axis=1)


def on_device(
    tokens, cotangent, norm1_gain, w_query, w_key, w_value, w_gate_out, w_out, w_beta, w_alpha,
    conv_query, conv_key, conv_value, a_log, dt_bias, head_gain, norm2_gain, w_up_gate, w_up,
    w_down,
):
    bf16, f32 = jnp.bfloat16, jnp.float32
    shard_rows, model = w_query.shape[0], tokens.shape[1]
    dp = model // shard_rows
    heads = a_log.shape[0]
    key_dim, value_dim = w_query.shape[1] // heads, w_value.shape[1] // heads
    taps = conv_query.shape[2]
    qk_width, v_width = heads * key_dim, heads * value_dim
    conv_width = 2 * qk_width + v_width
    hidden_width = w_up.shape[1]
    ff = round_up(hidden_width, 256)

    small_arrays = (norm1_gain, norm2_gain, conv_query, conv_key, conv_value, head_gain)
    small_cols = [as_columns(values, shard_rows) for values in small_arrays]
    counts = [cols.shape[1] for cols in small_cols]
    small = pad_columns(jnp.concatenate([w_beta, w_alpha] + small_cols, axis=1), LANES)
    mixer_pack = jnp.concatenate([w_query, w_key, w_value, w_gate_out, small, w_out], axis=1)
    in_width = conv_width + v_width + LANES
    rows_pack = jnp.concatenate([tokens, cotangent], axis=1)
    rows_full = lax.all_gather(rows_pack, "tensor", axis=0, tiled=True)
    mixer_full = lax.all_gather(mixer_pack, "dp", axis=0, tiled=True)
    ffn_pack = jnp.concatenate([pad_columns(w, ff) for w in (w_up_gate, w_up, w_down)], axis=1)
    mixer_full, ffn_pack = lax.optimization_barrier((mixer_full, ffn_pack))
    ffn_full = lax.all_gather(ffn_pack, "dp", axis=0, tiled=True)

    in_full = mixer_full[:, :in_width]
    out_full = mixer_full[:, in_width:]
    starts = [2 * heads]
    for count in counts:
        starts.append(starts[-1] + count)
    small_at = conv_width + v_width

    def unpacked(index):
        cols = mixer_full[:, small_at + starts[index] : small_at + starts[index + 1]]
        shape = small_arrays[index].shape
        size = small_arrays[index].size
        shards = cols.reshape(dp, -1)[:, :size]
        return shards.reshape((dp * shape[0],) + shape[1:]).astype(f32)

    gain_one, gain_two = unpacked(0), unpacked(1)
    conv_weights = jnp.concatenate([channel_weights(unpacked(i)) for i in (2, 3, 4)], axis=0)
    gain_row = unpacked(5).T.reshape(1, v_width)

    tokens_full = rows_full[:, :model].astype(f32)
    cot_full = rows_full[:, model:]
    _, unit_full = norm_forward(tokens_full)
    normed_one = (unit_full * gain_one).astype(bf16)
    projected = jnp.dot(normed_one, in_full, preferred_element_type=f32)
    proj_conv = projected[:, :conv_width]
    proj_gate = projected[:, conv_width:small_at]
    proj_beta = projected[:, small_at : small_at + heads]
    proj_alpha = projected[:, small_at + heads : small_at + 2 * heads]
    conv_all, conv_pull = jax.vjp(short_conv, proj_conv, conv_weights)
    rates, rates_pull = jax.vjp(
        rate_terms, proj_beta, proj_alpha, a_log.astype(f32), dt_bias.astype(f32)
    )
    mixed, states, inverses = mixer_forward(
        conv_all, proj_gate, rates, gain_row, heads, key_dim, value_dim
    )
    row_values = tokens.astype(f32)
    scale_one, unit_one = norm_forward(row_values)
    middle = row_values + lax.psum_scatter(
        times_transpose(mixed, out_full).astype(bf16), "tensor", scatter_dimension=0, tiled=True
    ).astype(f32)
    gates_full, down_full = ffn_full[:, : 2 * ff], ffn_full[:, 2 * ff :]
    grad_hidden = jnp.dot(cot_full, down_full, preferred_element_type=f32)
    scale_two, unit_two = norm_forward(middle)
    normed_two = lax.all_gather(
        (unit_two * gain_two).astype(bf16), "tensor", axis=0, tiled=True
    )
    ups = jnp.dot(normed_two, gates_full, preferred_element_type=f32)
    up_gate, up_lin = ups[:, :ff], ups[:, ff:]
    gate_sigmoid = jax.nn.sigmoid(up_gate)
    hidden = (up_gate * gate_sigmoid * up_lin).astype(bf16)
    grad_gate = (
        grad_hidden * up_lin * gate_sigmoid * (1.0 + up_gate * (1.0 - gate_sigmoid))
    ).astype(bf16)
    grad_lin = (grad_hidden * up_gate * gate_sigmoid).astype(bf16)
    grad_ups = jnp.concatenate([grad_gate, grad_lin], axis=1)
    grad_normed_two = lax.psum_scatter(
        times_transpose(grad_ups, gates_full).astype(bf16),
        "tensor",
        scatter_dimension=0,
        tiled=True,
    ).astype(f32)
    grad_gain_two = jnp.sum(grad_normed_two * unit_two, axis=0)
    grad_middle = cotangent.astype(f32) + norm_backward(
        grad_normed_two, unit_two, scale_two, gain_two
    )
    mid_full = lax.all_gather(grad_middle.astype(bf16), "tensor", axis=0, tiled=True)

    mid_full, hidden, grad_ups_late = lax.optimization_barrier((mid_full, hidden, grad_ups))
    ffn_grads = jnp.concatenate(
        [
            weight_grad(normed_two, grad_ups_late).astype(bf16),
            weight_grad(cot_full, hidden).astype(bf16),
            weight_grad(mid_full, mixed).astype(bf16),
        ],
        axis=1,
    )
    ffn_sums = lax.psum_scatter(ffn_grads, "dp", scatter_dimension=0, tiled=True).astype(f32)
    result = (
        middle
        + lax.psum_scatter(
            times_transpose(hidden, down_full).astype(bf16),
            "tensor",
            scatter_dimension=0,
            tiled=True,
        ).astype(f32)
    ).astype(bf16)

    grad_mixed = jnp.dot(mid_full, out_full, preferred_element_type=f32)
    grad_conv_all, grad_pgate, grad_rates, grad_gain_row = mixer_backward(
        conv_all, proj_gate, rates, gain_row, states, inverses, grad_mixed,
        heads, key_dim, value_dim,
    )
    grad_pconv, grad_conv_w = conv_pull(grad_conv_all)
    grad_beta, grad_alpha, grad_rate_part, grad_bias_part = rates_pull(grad_rates)
    grad_proj = jnp.concatenate(
        [
            grad_pconv.astype(bf16),
            grad_pgate.astype(bf16),
            pad_columns(
                jnp.concatenate([grad_beta.astype(bf16), grad_alpha.astype(bf16)], axis=1), LANES
            ),
        ],
        axis=1,
    )
    grad_normed_part = times_transpose(grad_proj, in_full)
    grad_normed_one = lax.psum_scatter(
        grad_normed_part.astype(bf16), "tensor", scatter_dimension=0, tiled=True
    ).astype(f32)
    grad_gain_one = jnp.sum(grad_normed_one * unit_one, axis=0)
    grad_rows = grad_middle + norm_backward(grad_normed_one, unit_one, scale_one, gain_one)

    def conv_grad(start, width, channels):
        part = grad_conv_w[start : start + width].reshape(heads, channels, taps)
        return jnp.swapaxes(part, 0, 1)

    conv_q_grad = conv_grad(0, qk_width, key_dim)
    conv_k_grad = conv_grad(qk_width, qk_width, key_dim)
    conv_v_grad = conv_grad(2 * qk_width, v_width, value_dim)
    head_gain_grad = grad_gain_row.reshape(heads, value_dim).T

    def grad_columns(values):
        shards = values.reshape(dp, -1)
        size = shards.shape[1]
        shards = jnp.pad(shards, ((0, 0), (0, round_up(size, shard_rows) - size)))
        return shards.reshape(model, -1)

    tail_cols = pad_columns(
        jnp.concatenate(
            [grad_columns(g) for g in (conv_q_grad, conv_k_grad, conv_v_grad, head_gain_grad)],
            axis=1,
        ),
        LANES,
    )
    mixer_grads = jnp.concatenate(
        [weight_grad(normed_one, grad_proj).astype(bf16), tail_cols.astype(bf16)], axis=1
    )
    mixer_sums = lax.psum_scatter(mixer_grads, "dp", scatter_dimension=0, tiled=True).astype(f32)

    head_total = heads * lax.axis_size("tensor")
    head_start = lax.axis_index("tensor") * heads

    def place_heads(local_grad):
        return lax.dynamic_update_slice(
            jnp.zeros((head_total,), f32), local_grad, (head_start,)
        )

    gain_parts = jnp.concatenate(
        [grad_gain_one, grad_gain_two, place_heads(grad_rate_part), place_heads(grad_bias_part)]
    )
    summed = lax.psum(gain_parts, ("dp", "tensor"))
    shard_start = lax.axis_index("dp") * shard_rows
    grad_gain_one_shard = lax.dynamic_slice_in_dim(summed, shard_start, shard_rows, 0)
    grad_gain_two_shard = lax.dynamic_slice_in_dim(summed, model + shard_start, shard_rows, 0)
    grad_rate = lax.dynamic_slice_in_dim(summed, 2 * model + head_start, heads, 0)
    grad_rate_bias = lax.dynamic_slice_in_dim(
        summed, 2 * model + head_total + head_start, heads, 0
    )

    def small_sum(index, at):
        shape, size = small_arrays[index].shape, small_arrays[index].size
        cols = mixer_sums[:, in_width + at : in_width + at + counts[index]]
        return cols.reshape(-1)[:size].reshape(shape)

    return (
        result,
        grad_rows,
        grad_gain_one_shard,
        mixer_sums[:, :qk_width],
        mixer_sums[:, qk_width : 2 * qk_width],
        mixer_sums[:, 2 * qk_width : conv_width],
        mixer_sums[:, conv_width:small_at],
        ffn_sums[:, 3 * ff :],
        mixer_sums[:, small_at : small_at + heads],
        mixer_sums[:, small_at + heads : small_at + 2 * heads],
        small_sum(2, 0),
        small_sum(3, counts[2]),
        small_sum(4, counts[2] + counts[3]),
        grad_rate,
        grad_rate_bias,
        small_sum(5, counts[2] + counts[3] + counts[4]),
        grad_gain_two_shard,
        ffn_sums[:, :hidden_width],
        ffn_sums[:, ff : ff + hidden_width],
        ffn_sums[:, 2 * ff : 2 * ff + hidden_width],
    )


def solution(mesh):
    placed = (
        P(("dp", "tensor"), None),
        P(("dp", "tensor"), None),
        P("dp"),
        P("dp", "tensor"),
        P("dp", "tensor"),
        P("dp", "tensor"),
        P("dp", "tensor"),
        P("dp", "tensor"),
        P("dp", "tensor"),
        P("dp", "tensor"),
        P("dp", "tensor", None),
        P("dp", "tensor", None),
        P("dp", "tensor", None),
        P("tensor"),
        P("tensor"),
        P("dp", "tensor"),
        P("dp"),
        P("dp", "tensor"),
        P("dp", "tensor"),
        P("dp", "tensor"),
    )
    return jax.shard_map(
        on_device,
        mesh=mesh,
        in_specs=placed,
        out_specs=(
            P(("dp", "tensor"), None),
            P(("dp", "tensor"), None),
            P("dp"),
            P("dp", "tensor"),
            P("dp", "tensor"),
            P("dp", "tensor"),
            P("dp", "tensor"),
            P("dp", "tensor"),
            P("dp", "tensor"),
            P("dp", "tensor"),
            P("dp", "tensor", None),
            P("dp", "tensor", None),
            P("dp", "tensor", None),
            P("tensor"),
            P("tensor"),
            P("dp", "tensor"),
            P("dp"),
            P("dp", "tensor"),
            P("dp", "tensor"),
            P("dp", "tensor"),
        ),
        check_vma=False,
    )
```

time: 2070 us -> 667 us (0.32)
  waiting for transfers between devices: 1130 us -> 431 us
  blocking collectives: 289 us -> 39.4 us
  other arithmetic: 270 us -> 36.5 us
  matrix products: 262 us -> 35.7 us
  Pallas kernels: 0 us -> 64.9 us
  local copies, waits for them, and re-layouts: 79.8 us -> 34.1 us
    reduce_scatter x12 -> x6, waiting for transfers between devices: 625 us -> 224 us  [the longest x1 106 us: on_device(): lax.psum_scatter(ffn_grads, 'dp', scatter_dimension=0, tiled=True)]
    unnamed x34 -> x11, waiting for transfers between devices: 331 us -> 0.7 us
    all_gather x10 -> x0, blocking collectives: 250 us -> none  [the longest x1 34.1 us: on_device(): lax.all_gather(w_query, 'dp', axis=0, tiled=True)]
    dot_general x162 -> x4, matrix products: 204 us -> 14.1 us  [the longest x1 4.18 us: on_device(): ups = jnp.dot(normed_two, gates_full, preferred_element_type=f32)]
    another operation x124 -> x3, other arithmetic: 176 us -> 1.11 us  [the longest x80 166 us: advance(): solved = solver(system, right_side)]
    pallas_call x0 -> x2, Pallas kernels: none -> 64.9 us  [the longest x1 32.7 us: mixer_forward(): pl.pallas_call(lambda *refs: mixer_forward_kernel(heads, key_dim, value_d...]
    dynamic_update_slice x57 -> x1, other arithmetic: 35.8 us -> 0.09 us  [place_heads(): lax.dynamic_update_slice(jnp.zeros((head_total,), f32), local_grad, (head...]
    all_gather x10 -> x5, waiting for transfers between devices: 173 us -> 207 us  [the longest x1 82.5 us: on_device(): ffn_full = lax.all_gather(ffn_pack, 'dp', axis=0, tiled=True)]
  transfers between devices with their start and end apart: 28 -> 11, of which waited for: 23 -> 10; matrix products, arithmetic and copies ran while one was open for 13% -> 6% of each run, Pallas kernels for 0% -> 0%
where the time goes in v1:
time: 667 us; the launch traced here: 658 us
  waiting for transfers between devices  431 us (65%)
  Pallas kernels  64.9 us (10%)
  blocking collectives  39.4 us (6%)
  other arithmetic  36.5 us (5%)
  matrix products  35.7 us (5%)
  local copies, waits for them, and re-layouts  34.1 us (5%)
  between operations  14.7 us (2%)
    reduce_scatter x1, waiting for transfers between devices, on_device(): lax.psum_scatter(ffn_grads, 'dp', scatter_dimension=0, tiled=True)  106 us
    all_gather x1, waiting for transfers between devices, on_device(): ffn_full = lax.all_gather(ffn_pack, 'dp', axis=0, tiled=True)  82.5 us
    all_gather x1, waiting for transfers between devices, on_device(): mixer_full = lax.all_gather(mixer_pack, 'dp', axis=0, tiled=True)  76.6 us
    reduce_scatter x1, waiting for transfers between devices, on_device(): lax.psum_scatter(mixer_grads, 'dp', scatter_dimension=0, tiled=True)  67.6 us
    psum x1, blocking collectives, on_device(): summed = lax.psum(gain_parts, ('dp', 'tensor'))  39.4 us
    pallas_call x1, Pallas kernels, mixer_forward(): pl.pallas_call(lambda *refs: mixer_forward_kernel(heads, key_dim, value_d...  32.7 us
    pallas_call x1, Pallas kernels, mixer_backward(): pl.pallas_call(lambda *refs: mixer_backward_kernel(heads, key_dim, value_...  32.3 us
    reduce_scatter x1, waiting for transfers between devices, on_device(): lax.psum_scatter(times_transpose(mixed, out_full).astype(bf16), 'tensor',...  23.4 us
  transfers between devices with their start and end apart: 11, of which 10 were waited for; matrix products, arithmetic and copies ran while one was open for 6% of the time, Pallas kernels for 0%

profile of v1, /device:TPU:0, one launch (start us, length us, event | category | flops | bytes accessed | tf_op | source)
XLA Modules:
  0.0 657.6 jit_solution(15043526797745027941)
XLA Ops:
  17.6 17.9 %all-gather.6.cloned.1.call-done = bf16[512,2048]{1,0:T(8,128)(2,1)} async-done(((bf16[128,2048]{1,0:T(8,128)(2,1)}), bf16[512,2048]{1,0:T(8,128)(2,1)}) %all-gather.6.cloned.1.call-update) | async-done | bytes 2097168 | tf_op jit(solution)/shard_map/all_gather | solution.py:332
  37.2 76.6 %all-gather.8.cloned.1.call-done = bf16[1024,2176]{1,0:T(8,128)(2,1)} async-done(((bf16[128,2176]{1,0:T(8,128)(2,1)}), bf16[1024,2176]{1,0:T(8,128)(2,1)}) %all-gather.8.cloned.1.call-update) | async-done | bytes 4456464 | tf_op jit(solution)/shard_map/all_gather | solution.py:333
  118.1 4.1 fusion.3
  130.4 32.7 %mixer_forward.1 = (bf16[512,512]{1,0:T(8,128)(2,1)}, f32[4,2,128,256]{3,2,1,0:T(8,128)}, f32[4,2,128,128]{3,2,1,0:T(8,128)}) custom-call(f32[512,1024]{1,0:T(8,128)} %multiply_add_fusion.refs_0_, f32[512,512]{1,0:T(8,128)} %slice.187.refs_1_, f32[512,4]{1,0:T(8,128)} %pad_maximum_fusion.4.refs_2_, f32[1,512]{1,0:T(1,128)} %bitcast.80), custom_call_target="tpu_custom_call" | custom-call | flops 8000000000 | bytes 8000000 | tf_op jit(solution)/shard_map/mixer_forward/pallas_call | solution.py:210
  163.0 3.2 convolution_convert_fusion.5
  166.3 23.4 %reduce-scatter.7.cloned.1.call-done = bf16[128,1024]{1,0:T(8,128)(2,1)} async-done(((bf16[512,1024]{1,0:T(8,128)(2,1)}), bf16[128,1024]{1,0:T(8,128)(2,1)}) %reduce-scatter.7.cloned.1.call-update) | async-done | bytes 262160 | tf_op jit(solution)/shard_map/reduce_scatter | solution.py:374
  193.5 15.9 %all-gather.12.cloned.1.call-done = bf16[512,1024]{1,0:T(8,128)(2,1)} async-done(((bf16[128,1024]{1,0:T(8,128)(2,1)}), bf16[512,1024]{1,0:T(8,128)(2,1)}) %all-gather.12.cloned.1.call-update) | async-done | bytes 1048592 | tf_op jit(solution)/shard_map/all_gather | solution.py:380
  209.4 82.5 %all-gather.10.cloned.1.call-done = bf16[1024,2304]{0,1:T(8,128)(2,1)} async-done(((bf16[128,2304]{0,1:T(8,128)(2,1)}), bf16[1024,2304]{0,1:T(8,128)(2,1)}) %all-gather.10.cloned.1.call-update) | async-done | bytes 4718608 | tf_op jit(solution)/shard_map/all_gather | solution.py:336
  291.9 4.2 fusion.7
  299.8 2.8 fusion.14
  302.7 23.1 %reduce-scatter.9.cloned.1.call-done = bf16[128,1024]{1,0:T(8,128)(2,1)} async-done(((bf16[512,1024]{1,0:T(8,128)(2,1)}), bf16[128,1024]{1,0:T(8,128)(2,1)}) %reduce-scatter.9.cloned.1.call-update) | async-done | bytes 262160 | tf_op jit(solution)/shard_map/reduce_scatter | solution.py:392
  329.2 2.7 pad_maximum_fusion.2
  331.9 13.9 %all-gather.14.cloned.1.call-done = bf16[512,1024]{1,0:T(8,128)(2,1)} async-done(((bf16[128,1024]{1,0:T(8,128)(2,1)}), bf16[512,1024]{1,0:T(8,128)(2,1)}) %all-gather.14.cloned.1.call-update) | async-done | bytes 1048592 | tf_op jit(solution)/shard_map/all_gather | solution.py:402
  345.8 3.3 fusion.29.refs_6_
  349.1 32.3 %mixer_backward.1 = (f32[512,1024]{1,0:T(8,128)}, f32[512,512]{1,0:T(8,128)}, f32[512,4]{1,0:T(8,128)}, f32[1,512]{1,0:T(1,128)}) custom-call(f32[512,1024]{1,0:T(8,128)} %multiply_add_fusion.refs_0_, f32[512,512]{1,0:T(8,128)} %slice.187.refs_1_, f32[512,4]{1,0:T(8,128)} %pad_maximum_fusion.4.refs_2_, f32[1,512]{1,0:T(1,128)} %bitcast.81, ...), custom_call_target="tpu_custom_call" | custom-call | flops 20000000000 | bytes 12000000 | tf_op jit(solution)/shard_map/mixer_backward/pallas_call | solution.py:244
  384.7 3.2 multiply_reduce_fusion.2
  389.0 5.1 fusion.17
  394.2 3.4 convolution_convert_fusion.3
  399.7 3.6 convolution_convert_fusion.1
  412.0 2.9 pad_maximum_fusion
  415.3 3.7 reduce-scatter.13.cloned.1.call-done
  420.4 39.4 %psum.7 = f32[2064]{0:T(1024)S(1)} all-reduce(f32[2064]{0:T(1024)S(1)} %concatenate.53), channel_id=1, replica_groups=mesh['dp'=8,'tensor'=4] {'dp','tensor'}, use_global_device_ids=true, to_apply=%region_13.14 | all-reduce | flops 2064 | bytes 16512 | tf_op jit(solution)/shard_map/psum | solution.py:486
  463.3 67.6 %reduce-scatter.15.cloned.1.call-done = bf16[128,1792]{1,0:T(8,128)(2,1)} async-done(((bf16[1024,1792]{1,0:T(8,128)(2,1)}), bf16[128,1792]{1,0:T(8,128)(2,1)}) %reduce-scatter.15.cloned.1.call-update) | async-done | bytes 458768 | tf_op jit(solution)/shard_map/reduce_scatter | solution.py:473
  539.4 106.0 %reduce-scatter.17.cloned.1.call-done = bf16[128,2816]{1,0:T(8,128)(2,1)} async-done(((bf16[1024,2816]{1,0:T(8,128)(2,1)}), bf16[128,2816]{1,0:T(8,128)(2,1)}) %reduce-scatter.17.cloned.1.call-update) | async-done | bytes 720912 | tf_op jit(solution)/shard_map/reduce_scatter | solution.py:413
  (194 shorter events, 69.6 us)
Async XLA Ops:
  7.2 8.5 %copy-start.17 = (bf16[128,512]{1,0:T(8,128)(2,1)S(1)}, bf16[128,512]{1,0:T(8,128)(2,1)}, u32[]{:S(2)}) copy-start(bf16[128,512]{1,0:T(8,128)(2,1)} %param.25) | copy-start | bytes 393220
  7.2 8.5 %copy-start.18 = (bf16[128,512]{1,0:T(8,128)(2,1)S(1)}, bf16[128,512]{1,0:T(8,128)(2,1)}, u32[]{:S(2)}) copy-start(bf16[128,512]{1,0:T(8,128)(2,1)} %param.26) | copy-start | bytes 393220
  7.2 8.5 %copy-start.19 = (bf16[128,512]{1,0:T(8,128)(2,1)S(1)}, bf16[128,512]{1,0:T(8,128)(2,1)}, u32[]{:S(2)}) copy-start(bf16[128,512]{1,0:T(8,128)(2,1)} %param.27) | copy-start | bytes 393220
  7.2 9.5 %copy-start.25 = (bf16[2]{0:T(256)(128)(2,1)S(1)}, bf16[2]{0:T(256)(128)(2,1)}, u32[]{:S(2)}) copy-start(bf16[2]{0:T(256)(128)(2,1)} %param.34) | copy-start | bytes 16
  7.2 9.5 %copy-start.21 = (bf16[2]{0:T(256)(128)(2,1)S(1)}, bf16[2]{0:T(256)(128)(2,1)}, u32[]{:S(2)}) copy-start(bf16[2]{0:T(256)(128)(2,1)} %param.33) | copy-start | bytes 16
  7.2 9.5 %copy-start.14 = (bf16[128,704]{0,1:T(8,128)(2,1)S(1)}, bf16[128,704]{0,1:T(8,128)(2,1)}, u32[]{:S(2)}) copy-start(bf16[128,704]{0,1:T(8,128)(2,1)} %param.39) | copy-start | bytes 540676
  7.3 9.5 %copy-start.15 = (bf16[128,704]{0,1:T(8,128)(2,1)S(1)}, bf16[128,704]{0,1:T(8,128)(2,1)}, u32[]{:S(2)}) copy-start(bf16[128,704]{0,1:T(8,128)(2,1)} %param.38) | copy-start | bytes 540676
  7.3 9.5 %copy-start.16 = (bf16[128,704]{0,1:T(8,128)(2,1)S(1)}, bf16[128,704]{0,1:T(8,128)(2,1)}, u32[]{:S(2)}) copy-start(bf16[128,704]{0,1:T(8,128)(2,1)} %param.37) | copy-start | bytes 540676
  7.3 28.3 %all-gather.6.cloned.1.call-start = ((), (), s32[]{:S(2)}) async-start(), calls=%async_computation.6 | async-start | bytes 2621440 | tf_op jit(solution)/shard_map/all_gather | solution.py:332
  9.4 104.4 %all-gather.8.cloned.1.call-start = ((), (), s32[]{:S(2)}) async-start(), calls=%async_computation.7 | async-start | bytes 5013504 | tf_op jit(solution)/shard_map/all_gather | solution.py:333
  16.6 173.0 %reduce-scatter.7.cloned.1.call-start = ((), (), s32[]{:S(2)}) async-start(), calls=%async_computation.8 | async-start | bytes 1310720 | tf_op jit(solution)/shard_map/reduce_scatter | solution.py:374
  35.5 82.5 %copy-start.11 = (bf16[512,2048]{1,0:T(8,128)(2,1)S(1)}, bf16[512,2048]{1,0:T(8,128)(2,1)}, u32[]{:S(2)}) copy-start(bf16[512,2048]{1,0:T(8,128)(2,1)} %all-gather.6.cloned.1.call-done) | copy-start | bytes 6291460
  163.0 26.6 %copy-start = (bf16[128,1024]{1,0:T(8,128)(2,1)S(1)}, bf16[128,1024]{1,0:T(8,128)(2,1)}, u32[]{:S(2)}) copy-start(bf16[128,1024]{1,0:T(8,128)(2,1)} %param.20) | copy-start | bytes 786436
  166.2 43.2 %all-gather.12.cloned.1.call-start = ((), (), s32[]{:S(2)}) async-start(), calls=%async_computation.10 | async-start | bytes 1310720 | tf_op jit(solution)/shard_map/all_gather | solution.py:380
  192.5 99.4 %all-gather.10.cloned.1.call-start = ((), (), s32[]{:S(2)}) async-start(), calls=%async_computation.9 | async-start | bytes 5308416 | tf_op jit(solution)/shard_map/all_gather | solution.py:336
  193.1 132.6 %reduce-scatter.9.cloned.1.call-start = ((), (), s32[]{:S(2)}) async-start(), calls=%async_computation.11 | async-start | bytes 1310720 | tf_op jit(solution)/shard_map/reduce_scatter | solution.py:392
  299.8 26.0 %copy-start.2 = (bf16[128,1024]{1,0:T(8,128)(2,1)S(1)}, bf16[128,1024]{1,0:T(8,128)(2,1)}, u32[]{:S(2)}) copy-start(bf16[128,1024]{1,0:T(8,128)(2,1)} %reduce-scatter.7.cloned.1.call-done) | copy-start | bytes 786436
  299.8 27.2 %copy-start.5 = (bf16[128,1024]{1,0:T(8,128)(2,1)S(1)}, bf16[128,1024]{1,0:T(8,128)(2,1)}, u32[]{:S(2)}) copy-start(bf16[128,1024]{1,0:T(8,128)(2,1)} %param.21) | copy-start | bytes 786436
  302.6 43.2 %all-gather.14.cloned.1.call-start = ((), (), s32[]{:S(2)}) async-start(), calls=%async_computation.12 | async-start | bytes 1310720 | tf_op jit(solution)/shard_map/all_gather | solution.py:402
  329.0 90.1 %reduce-scatter.13.cloned.1.call-start = ((), (), s32[]{:S(2)}) async-start(), calls=%async_computation.14 | async-start | bytes 1310720 | tf_op jit(solution)/shard_map/reduce_scatter | solution.py:442
  394.1 66.9 %reduce-scatter.11.cloned.1.call-start = ((), (), s32[]{:S(2)}) async-start(), calls=%async_computation.13 | async-start | bytes 1310720 | tf_op jit(solution)/shard_map/reduce_scatter | solution.py:416
  397.6 133.4 %reduce-scatter.15.cloned.1.call-start = ((), (), s32[]{:S(2)}) async-start(), calls=%async_computation.15 | async-start | bytes 4128768 | tf_op jit(solution)/shard_map/reduce_scatter | solution.py:473
  405.5 239.9 %reduce-scatter.17.cloned.1.call-start = ((), (), s32[]{:S(2)}) async-start(), calls=%async_computation.16 | async-start | bytes 6488064 | tf_op jit(solution)/shard_map/reduce_scatter | solution.py:413
  414.9 46.1 %copy-start.4 = (bf16[128,1024]{1,0:T(8,128)(2,1)S(1)}, bf16[128,1024]{1,0:T(8,128)(2,1)}, u32[]{:S(2)}) copy-start(bf16[128,1024]{1,0:T(8,128)(2,1)} %reduce-scatter.9.cloned.1.call-done) | copy-start | bytes 786436
  (16 other events, 42.9 us)
Sparse Core Ops, SparseCore 0:
  10.2 25.2 all-gather.5
  37.7 76.0 all-gather.7
  166.3 23.2 reduce-scatter.6
  192.7 16.6 all-gather.11
  211.3 80.5 all-gather.9
  302.7 22.9 reduce-scatter.8
  329.1 16.6 all-gather.13
  394.2 24.8 reduce-scatter.12
  421.6 24.8 reduce-scatter.10
  449.9 80.9 reduce-scatter.14
  534.6 110.7 reduce-scatter.16

commit v2 on v1

--- a/solution.py
+++ b/solution.py
@@ -229,7 +229,7 @@
         ],
         scratch_shapes=[pltpu.VMEM((heads, key_dim, value_dim), jnp.float32)],
         cost_estimate=pl.CostEstimate(
-            flops=80_000_000_00, bytes_accessed=8_000_000, transcendentals=1_000_000
+            flops=30_000_000_000, bytes_accessed=8_000_000, transcendentals=1_000_000
         ),
     )(conv_all, proj_gate, rates, gain_row)
 
@@ -268,9 +268,68 @@
         ],
         scratch_shapes=[pltpu.VMEM((heads, key_dim, value_dim), jnp.float32)],
         cost_estimate=pl.CostEstimate(
-            flops=200_000_000_00, bytes_accessed=12_000_000, transcendentals=2_000_000
+            flops=30_000_000_000, bytes_accessed=12_000_000, transcendentals=2_000_000
         ),
     )(conv_all, proj_gate, rates, gain_row, states, inverses, grad_gated)
+
+
+def exchange_kernel(axis, ranks, scatter, block_ref, got_ref, send_sems, recv_sems):
+    me = lax.axis_index(axis)
+    barrier = pltpu.get_barrier_semaphore()
+    for step in range(1, ranks):
+        pl.semaphore_signal(
+            barrier,
+            inc=1,
+            device_id={axis: lax.rem(me + step, ranks)},
+            device_id_type=pl.DeviceIdType.MESH,
+        )
+    pl.semaphore_wait(barrier, ranks - 1)
+    copies = []
+    for step in range(1, ranks):
+        peer = lax.rem(me + step, ranks)
+        copy = pltpu.make_async_remote_copy(
+            src_ref=block_ref.at[peer] if scatter else block_ref.at[0],
+            dst_ref=got_ref.at[me],
+            send_sem=send_sems.at[step - 1],
+            recv_sem=recv_sems.at[step - 1],
+            device_id={axis: peer},
+            device_id_type=pl.DeviceIdType.MESH,
+        )
+        copy.start()
+        copies.append(copy)
+    got_ref[me] = block_ref[me] if scatter else block_ref[0]
+    for copy in copies:
+        copy.wait()
+
+
+def exchange(blocks, axis, number, scatter):
+    ranks = lax.axis_size(axis)
+    return pl.pallas_call(
+        lambda *refs: exchange_kernel(axis, ranks, scatter, *refs),
+        name="exchange",
+        in_specs=[pl.BlockSpec(memory_space=pltpu.VMEM)],
+        out_specs=pl.BlockSpec(memory_space=pltpu.VMEM),
+        out_shape=jax.ShapeDtypeStruct((ranks,) + blocks.shape[1:], blocks.dtype),
+        scratch_shapes=[
+            pltpu.SemaphoreType.DMA((ranks - 1,)),
+            pltpu.SemaphoreType.DMA((ranks - 1,)),
+        ],
+        compiler_params=pltpu.CompilerParams(collective_id=number, has_side_effects=True),
+        cost_estimate=pl.CostEstimate(
+            flops=10_000_000_000, bytes_accessed=blocks.size * 4, transcendentals=0
+        ),
+    )(blocks)
+
+
+def gather_rows(block, axis, number):
+    got = exchange(block[None], axis, number, False)
+    return got.reshape(-1, block.shape[1])
+
+
+def scatter_sum(partial, axis, number):
+    ranks = lax.axis_size(axis)
+    got = exchange(partial.reshape(ranks, -1, partial.shape[1]), axis, number, True)
+    return jnp.sum(got.astype(jnp.float32), axis=0)
 
 
 def short_conv(inputs, weights):
@@ -329,7 +388,7 @@
     mixer_pack = jnp.concatenate([w_query, w_key, w_value, w_gate_out, small, w_out], axis=1)
     in_width = conv_width + v_width + LANES
     rows_pack = jnp.concatenate([tokens, cotangent], axis=1)
-    rows_full = lax.all_gather(rows_pack, "tensor", axis=0, tiled=True)
+    rows_full = gather_rows(rows_pack, "tensor", 1)
     mixer_full = lax.all_gather(mixer_pack, "dp", axis=0, tiled=True)
     ffn_pack = jnp.concatenate([pad_columns(w, ff) for w in (w_up_gate, w_up, w_down)], axis=1)
     mixer_full, ffn_pack = lax.optimization_barrier((mixer_full, ffn_pack))
@@ -371,15 +430,13 @@
     )
     row_values = tokens.astype(f32)
     scale_one, unit_one = norm_forward(row_values)
-    middle = row_values + lax.psum_scatter(
-        times_transpose(mixed, out_full).astype(bf16), "tensor", scatter_dimension=0, tiled=True
-    ).astype(f32)
+    middle = row_values + scatter_sum(
+        times_transpose(mixed, out_full).astype(bf16), "tensor", 2
+    )
     gates_full, down_full = ffn_full[:, : 2 * ff], ffn_full[:, 2 * ff :]
     grad_hidden = jnp.dot(cot_full, down_full, preferred_element_type=f32)
     scale_two, unit_two = norm_forward(middle)
-    normed_two = lax.all_gather(
-        (unit_two * gain_two).astype(bf16), "tensor", axis=0, tiled=True
-    )
+    normed_two = gather_rows((unit_two * gain_two).astype(bf16), "tensor", 3)
     ups = jnp.dot(normed_two, gates_full, preferred_element_type=f32)
     up_gate, up_lin = ups[:, :ff], ups[:, ff:]
     gate_sigmoid = jax.nn.sigmoid(up_gate)
@@ -389,36 +446,29 @@
     ).astype(bf16)
     grad_lin = (grad_hidden * up_gate * gate_sigmoid).astype(bf16)
     grad_ups = jnp.concatenate([grad_gate, grad_lin], axis=1)
-    grad_normed_two = lax.psum_scatter(
-        times_transpose(grad_ups, gates_full).astype(bf16),
-        "tensor",
-        scatter_dimension=0,
-        tiled=True,
-    ).astype(f32)
+    grad_normed_two = scatter_sum(
+        times_transpose(grad_ups, gates_full).astype(bf16), "tensor", 4
+    )
+    ffn_grads = jnp.concatenate(
+        [
+            weight_grad(normed_two, grad_ups).astype(bf16),
+            weight_grad(cot_full, hidden).astype(bf16),
+        ],
+        axis=1,
+    )
+    grad_normed_two, ffn_grads = lax.optimization_barrier((grad_normed_two, ffn_grads))
+    ffn_sums = lax.psum_scatter(ffn_grads, "dp", scatter_dimension=0, tiled=True)
     grad_gain_two = jnp.sum(grad_normed_two * unit_two, axis=0)
     grad_middle = cotangent.astype(f32) + norm_backward(
         grad_normed_two, unit_two, scale_two, gain_two
     )
-    mid_full = lax.all_gather(grad_middle.astype(bf16), "tensor", axis=0, tiled=True)
-
-    mid_full, hidden, grad_ups_late = lax.optimization_barrier((mid_full, hidden, grad_ups))
-    ffn_grads = jnp.concatenate(
-        [
-            weight_grad(normed_two, grad_ups_late).astype(bf16),
-            weight_grad(cot_full, hidden).astype(bf16),
-            weight_grad(mid_full, mixed).astype(bf16),
-        ],
-        axis=1,
-    )
-    ffn_sums = lax.psum_scatter(ffn_grads, "dp", scatter_dimension=0, tiled=True).astype(f32)
+    mid_full = gather_rows(grad_middle.astype(bf16), "tensor", 5)
+    out_grads = weight_grad(mid_full, mixed).astype(bf16)
+    out_grads, mid_full = lax.optimization_barrier((out_grads, mid_full))
+    out_grads, ffn_sums = lax.optimization_barrier((out_grads, ffn_sums))
+    out_sums = lax.psum_scatter(out_grads, "dp", scatter_dimension=0, tiled=True)
     result = (
-        middle
-        + lax.psum_scatter(
-            times_transpose(hidden, down_full).astype(bf16),
-            "tensor",
-            scatter_dimension=0,
-            tiled=True,
-        ).astype(f32)
+        middle + scatter_sum(times_transpose(hidden, down_full).astype(bf16), "tensor", 6)
     ).astype(bf16)
 
     grad_mixed = jnp.dot(mid_full, out_full, preferred_element_type=f32)
@@ -439,10 +489,20 @@
         axis=1,
     )
     grad_normed_part = times_transpose(grad_proj, in_full)
-    grad_normed_one = lax.psum_scatter(
-        grad_normed_part.astype(bf16), "tensor", scatter_dimension=0, tiled=True
-    ).astype(f32)
-    grad_gain_one = jnp.sum(grad_normed_one * unit_one, axis=0)
+    ranks = lax.axis_size("tensor")
+    gain_lines = jnp.stack([jnp.sum(grad_normed_part * unit_full, axis=0), grad_gain_two])
+    gain_lines = jnp.pad(gain_lines, ((0, 14), (0, 0))).astype(bf16)
+    sent = jnp.concatenate(
+        [
+            grad_normed_part.astype(bf16).reshape(ranks, -1, model),
+            jnp.broadcast_to(gain_lines, (ranks,) + gain_lines.shape),
+        ],
+        axis=1,
+    )
+    received = scatter_sum(sent.reshape(-1, model), "tensor", 7)
+    own_rows = tokens.shape[0]
+    grad_normed_one = received[:own_rows]
+    gain_columns = received[own_rows : own_rows + 2].T
     grad_rows = grad_middle + norm_backward(grad_normed_one, unit_one, scale_one, gain_one)
 
     def conv_grad(start, width, channels):
@@ -460,9 +520,13 @@
         shards = jnp.pad(shards, ((0, 0), (0, round_up(size, shard_rows) - size)))
         return shards.reshape(model, -1)
 
+    rate_line = jnp.concatenate([grad_rate_part, grad_bias_part])
+    rate_tile = jnp.pad(rate_line[None], ((0, 7), (0, LANES - 2 * heads)))
+    rate_sums = jnp.sum(exchange(rate_tile[None], "dp", 8, False), axis=0)[0]
     tail_cols = pad_columns(
         jnp.concatenate(
-            [grad_columns(g) for g in (conv_q_grad, conv_k_grad, conv_v_grad, head_gain_grad)],
+            [grad_columns(g) for g in (conv_q_grad, conv_k_grad, conv_v_grad, head_gain_grad)]
+            + [gain_columns],
             axis=1,
         ),
         LANES,
@@ -470,27 +534,12 @@
     mixer_grads = jnp.concatenate(
         [weight_grad(normed_one, grad_proj).astype(bf16), tail_cols.astype(bf16)], axis=1
     )
+    mixer_grads, out_sums = lax.optimization_barrier((mixer_grads, out_sums))
     mixer_sums = lax.psum_scatter(mixer_grads, "dp", scatter_dimension=0, tiled=True).astype(f32)
-
-    head_total = heads * lax.axis_size("tensor")
-    head_start = lax.axis_index("tensor") * heads
-
-    def place_heads(local_grad):
-        return lax.dynamic_update_slice(
-            jnp.zeros((head_total,), f32), local_grad, (head_start,)
-        )
-
-    gain_parts = jnp.concatenate(
-        [grad_gain_one, grad_gain_two, place_heads(grad_rate_part), place_heads(grad_bias_part)]
-    )
-    summed = lax.psum(gain_parts, ("dp", "tensor"))
-    shard_start = lax.axis_index("dp") * shard_rows
-    grad_gain_one_shard = lax.dynamic_slice_in_dim(summed, shard_start, shard_rows, 0)
-    grad_gain_two_shard = lax.dynamic_slice_in_dim(summed, model + shard_start, shard_rows, 0)
-    grad_rate = lax.dynamic_slice_in_dim(summed, 2 * model + head_start, heads, 0)
-    grad_rate_bias = lax.dynamic_slice_in_dim(
-        summed, 2 * model + head_total + head_start, heads, 0
-    )
+    out_sums, ffn_sums = out_sums.astype(f32), ffn_sums.astype(f32)
+    small_end = in_width + sum(counts[2:])
+    grad_rate = rate_sums[:heads]
+    grad_rate_bias = rate_sums[heads : 2 * heads]
 
     def small_sum(index, at):
         shape, size = small_arrays[index].shape, small_arrays[index].size
@@ -500,12 +549,12 @@
     return (
         result,
         grad_rows,
-        grad_gain_one_shard,
+        mixer_sums[:, small_end],
         mixer_sums[:, :qk_width],
         mixer_sums[:, qk_width : 2 * qk_width],
         mixer_sums[:, 2 * qk_width : conv_width],
         mixer_sums[:, conv_width:small_at],
-        ffn_sums[:, 3 * ff :],
+        out_sums,
         mixer_sums[:, small_at : small_at + heads],
         mixer_sums[:, small_at + heads : small_at + 2 * heads],
         small_sum(2, 0),
@@ -514,7 +563,7 @@
         grad_rate,
         grad_rate_bias,
         small_sum(5, counts[2] + counts[3] + counts[4]),
-        grad_gain_two_shard,
+        mixer_sums[:, small_end + 1],
         ffn_sums[:, :hidden_width],
         ffn_sums[:, ff : ff + hidden_width],
         ffn_sums[:, 2 * ff : 2 * ff + hidden_width],

time: 667 us -> 492 us (0.74)
  waiting for transfers between devices: 431 us -> 146 us
  Pallas kernels: 64.9 us -> 197 us
  blocking collectives: 39.4 us -> 0 us
  other arithmetic: 36.5 us -> 47.6 us
    pallas_call x0 -> x8, Pallas kernels: none -> 132 us  [exchange(): pl.pallas_call(lambda *refs: exchange_kernel(axis, ranks, scatter, *refs)...]
    reduce_scatter x1, waiting for transfers between devices: 106 us -> 9.69 us  [on_device(): lax.psum_scatter(ffn_grads, 'dp', scatter_dimension=0, tiled=True)]
    all_gather x1, waiting for transfers between devices: 82.5 us -> 0.02 us  [on_device(): ffn_full = lax.all_gather(ffn_pack, 'dp', axis=0, tiled=True)]
    all_gather x3 -> x0, waiting for transfers between devices: 47.7 us -> none  [the longest x1 17.9 us: on_device(): rows_full = lax.all_gather(rows_pack, 'tensor', axis=0, tiled=True)]
    psum x1 -> x0, blocking collectives: 39.4 us -> none  [on_device(): summed = lax.psum(gain_parts, ('dp', 'tensor'))]
    all_gather x1, waiting for transfers between devices: 76.6 us -> 46.4 us  [on_device(): mixer_full = lax.all_gather(mixer_pack, 'dp', axis=0, tiled=True)]
    reduce_scatter x1, waiting for transfers between devices: 67.6 us -> 48 us  [on_device(): lax.psum_scatter(mixer_grads, 'dp', scatter_dimension=0, tiled=True)]
    reduce_scatter x4 -> x1, waiting for transfers between devices: 50.2 us -> 42.2 us  [on_device(): lax.psum_scatter(out_grads, 'dp', scatter_dimension=0, tiled=True)]
  transfers between devices with their start and end apart: 11 -> 5, of which waited for: 10 -> 4; matrix products, arithmetic and copies ran while one was open for 6% -> 17% of each run, Pallas kernels for 0% -> 38%
where the time goes in v2:
time: 492 us; the launch traced here: 483 us
  Pallas kernels  197 us (40%)
  waiting for transfers between devices  146 us (30%)
  other arithmetic  47.6 us (10%)
  matrix products  40.5 us (8%)
  local copies, waits for them, and re-layouts  35.3 us (7%)
  between operations  15 us (3%)
    pallas_call x8, Pallas kernels, exchange(): pl.pallas_call(lambda *refs: exchange_kernel(axis, ranks, scatter, *refs)...  132 us
    reduce_scatter x1, waiting for transfers between devices, on_device(): lax.psum_scatter(mixer_grads, 'dp', scatter_dimension=0, tiled=True)  48 us
    all_gather x1, waiting for transfers between devices, on_device(): mixer_full = lax.all_gather(mixer_pack, 'dp', axis=0, tiled=True)  46.4 us
    reduce_scatter x1, waiting for transfers between devices, on_device(): lax.psum_scatter(out_grads, 'dp', scatter_dimension=0, tiled=True)  42.2 us
    pallas_call x1, Pallas kernels, mixer_forward(): pl.pallas_call(lambda *refs: mixer_forward_kernel(heads, key_dim, value_d...  32.8 us
    pallas_call x1, Pallas kernels, mixer_backward(): pl.pallas_call(lambda *refs: mixer_backward_kernel(heads, key_dim, value_...  32.6 us
    unnamed x101, local copies, waits for them, and re-layouts  17.1 us
    dot_general x4, matrix products, times_transpose(): lax.dot_general(left_in, right_in, contract_cols, preferred_element_type=...  13.6 us
  transfers between devices with their start and end apart: 5, of which 4 were waited for; matrix products, arithmetic and copies ran while one was open for 17% of the time, Pallas kernels for 38%

profile of v2, /device:TPU:0, one launch (start us, length us, event | category | flops | bytes accessed | tf_op | source)
XLA Modules:
  0.0 482.7 jit_solution(9225088684114776610)
XLA Ops:
  21.4 28.4 %exchange.8 = bf16[4,128,2048]{2,1,0:T(8,128)(2,1)} custom-call(bf16[1,128,2048]{2,1,0:T(8,128)(2,1)} %maximum_bitcast_fusion.refs_0_), custom_call_target="tpu_custom_call" | custom-call | flops 10000000000 | bytes 1048576 | tf_op jit(solution)/shard_map/exchange/pallas_call | solution.py:307
  49.8 46.4 %all-gather.3.cloned.1.call-done = bf16[1024,2176]{1,0:T(8,128)(2,1)} async-done(((bf16[128,2176]{1,0:T(8,128)(2,1)}), bf16[1024,2176]{1,0:T(8,128)(2,1)}) %all-gather.3.cloned.1.call-update) | async-done | bytes 4456464 | tf_op jit(solution)/shard_map/all_gather | solution.py:392
  100.3 4.1 fusion.5
  115.2 32.8 %mixer_forward.1 = (bf16[512,512]{1,0:T(8,128)(2,1)}, f32[4,2,128,256]{3,2,1,0:T(8,128)}, f32[4,2,128,128]{3,2,1,0:T(8,128)}) custom-call(f32[512,1024]{1,0:T(8,128)} %multiply_add_fusion.refs_0_, f32[512,512]{1,0:T(8,128)} %slice.219.refs_1_, f32[512,4]{1,0:T(8,128)} %pad_maximum_fusion.5.refs_2_, f32[1,512]{1,0:T(1,128)} %bitcast.108), custom_call_target="tpu_custom_call" | custom-call | flops 30000001024 | bytes 8000000 | tf_op jit(solution)/shard_map/mixer_forward/pallas_call | solution.py:210
  148.1 3.1 convolution_convert_fusion.5
  151.2 15.6 %exchange.9 = bf16[4,128,1024]{2,1,0:T(8,128)(2,1)} custom-call(bf16[4,128,1024]{2,1,0:T(8,128)(2,1)} %bitcast.118), custom_call_target="tpu_custom_call" | custom-call | flops 10000000000 | bytes 2097152 | tf_op jit(solution)/shard_map/exchange/pallas_call | solution.py:307
  169.8 16.1 %exchange.10 = bf16[4,128,1024]{2,1,0:T(8,128)(2,1)} custom-call(bf16[1,128,1024]{2,1,0:T(8,128)(2,1)} %fusion.44.refs_0_), custom_call_target="tpu_custom_call" | custom-call | flops 10000000000 | bytes 524288 | tf_op jit(solution)/shard_map/exchange/pallas_call | solution.py:307
  185.9 4.2 fusion.9
  192.6 3.5 convolution_convert_fusion.1
  199.0 15.9 %exchange.12 = bf16[4,128,1024]{2,1,0:T(8,128)(2,1)} custom-call(bf16[4,128,1024]{2,1,0:T(8,128)(2,1)} %bitcast.116), custom_call_target="tpu_custom_call" | custom-call | flops 10000000000 | bytes 2097152 | tf_op jit(solution)/shard_map/exchange/pallas_call | solution.py:307
  226.4 15.7 %exchange.13 = bf16[4,128,1024]{2,1,0:T(8,128)(2,1)} custom-call(bf16[1,128,1024]{2,1,0:T(8,128)(2,1)} %convert_bitcast_fusion.refs_0_), custom_call_target="tpu_custom_call" | custom-call | flops 10000000000 | bytes 524288 | tf_op jit(solution)/shard_map/exchange/pallas_call | solution.py:307
  245.2 3.3 fusion.30.refs_6_
  248.6 32.6 %mixer_backward.1 = (f32[512,1024]{1,0:T(8,128)}, f32[512,512]{1,0:T(8,128)}, f32[512,4]{1,0:T(8,128)}, f32[1,512]{1,0:T(1,128)}) custom-call(f32[512,1024]{1,0:T(8,128)} %multiply_add_fusion.refs_0_, f32[512,512]{1,0:T(8,128)} %slice.219.refs_1_, f32[512,4]{1,0:T(8,128)} %pad_maximum_fusion.5.refs_2_, f32[1,512]{1,0:T(1,128)} %bitcast.109, ...), custom_call_target="tpu_custom_call" | custom-call | flops 30000001024 | bytes 12000000 | tf_op jit(solution)/shard_map/mixer_backward/pallas_call | solution.py:244
  289.0 5.3 %multiply_reduce_fusion.2 = (f32[1024]{0:T(1024)S(1)}, f32[1024]{0:T(1024)S(1)}, f32[1024]{0:T(1024)S(1)}, f32[1024]{0:T(1024)S(1)}, f32[512,1024]{1,0:T(8,128)}...) fusion(f32[512,1024]{1,0:T(8,128)} %get-tuple-element.44, f32[512,1024]{1,0:T(8,128)S(1)} %slice.214, ...), kind=kLoop, calls=%fused_computation.30 | loop fusion | flops 6287360 | bytes 14712832 | tf_op jit(solution)/shard_map/transpose(jvp())/reduce_sum | solution.py:341
  296.6 4.7 fusion.16
  301.3 4.1 fusion.71
  306.6 9.7 %reduce-scatter.4.cloned.1.call-done = bf16[128,2304]{1,0:T(8,128)(2,1)} async-done(((bf16[1024,2304]{1,0:T(8,128)(2,1)}), bf16[128,2304]{1,0:T(8,128)(2,1)}) %reduce-scatter.4.cloned.1.call-update) | async-done | bytes 589840 | tf_op jit(solution)/shard_map/reduce_scatter | solution.py:460
  316.7 17.0 %exchange.14 = bf16[4,144,1024]{2,1,0:T(8,128)(2,1)} custom-call(bf16[4,144,1024]{2,1,0:T(8,128)(2,1)} %pad_maximum_fusion.2.refs_0_), custom_call_target="tpu_custom_call" | custom-call | flops 10000000000 | bytes 2359296 | tf_op jit(solution)/shard_map/exchange/pallas_call | solution.py:307
  335.5 3.6 convolution_convert_fusion
  341.2 42.2 %reduce-scatter.6.cloned.1.call-done = bf16[128,512]{1,0:T(8,128)(2,1)} async-done(((bf16[1024,512]{1,0:T(8,128)(2,1)}), bf16[128,512]{1,0:T(8,128)(2,1)}) %reduce-scatter.6.cloned.1.call-update) | async-done | bytes 131088 | tf_op jit(solution)/shard_map/reduce_scatter | solution.py:469
  384.2 7.8 %exchange.15 = f32[8,8,128]{2,1,0:T(8,128)} custom-call(f32[1,8,128]{2,1,0:T(8,128)} %pad_bitcast_fusion.refs_0_), custom_call_target="tpu_custom_call" | custom-call | flops 10000000000 | bytes 4096 | tf_op jit(solution)/shard_map/exchange/pallas_call | solution.py:307
  393.0 3.5 convolution_convert_fusion.3
  396.5 15.6 %exchange.11 = bf16[4,128,1024]{2,1,0:T(8,128)(2,1)} custom-call(bf16[4,128,1024]{2,1,0:T(8,128)(2,1)} %bitcast.117), custom_call_target="tpu_custom_call" | custom-call | flops 10000000000 | bytes 2097152 | tf_op jit(solution)/shard_map/exchange/pallas_call | solution.py:307
  418.8 48.0 %reduce-scatter.8.cloned.1.call-done = bf16[128,1792]{1,0:T(8,128)(2,1)} async-done(((bf16[1024,1792]{1,0:T(8,128)(2,1)}), bf16[128,1792]{1,0:T(8,128)(2,1)}) %reduce-scatter.8.cloned.1.call-update) | async-done | bytes 458768 | tf_op jit(solution)/shard_map/reduce_scatter | solution.py:538
  (211 shorter events, 84.6 us)
Async XLA Ops:
  7.2 13.3 %copy-start.12 = (bf16[128,704]{0,1:T(8,128)(2,1)S(1)}, bf16[128,704]{0,1:T(8,128)(2,1)}, u32[]{:S(2)}) copy-start(bf16[128,704]{0,1:T(8,128)(2,1)} %param.39) | copy-start | bytes 540676
  7.2 13.3 %copy-start.13 = (bf16[128,704]{0,1:T(8,128)(2,1)S(1)}, bf16[128,704]{0,1:T(8,128)(2,1)}, u32[]{:S(2)}) copy-start(bf16[128,704]{0,1:T(8,128)(2,1)} %param.38) | copy-start | bytes 540676
  7.2 13.3 %copy-start.14 = (bf16[128,704]{0,1:T(8,128)(2,1)S(1)}, bf16[128,704]{0,1:T(8,128)(2,1)}, u32[]{:S(2)}) copy-start(bf16[128,704]{0,1:T(8,128)(2,1)} %param.37) | copy-start | bytes 540676
  7.2 88.9 %all-gather.3.cloned.1.call-start = ((), (), s32[]{:S(2)}) async-start(), calls=%async_computation.3 | async-start | bytes 5013504 | tf_op jit(solution)/shard_map/all_gather | solution.py:392
  17.2 168.6 %all-gather.5.cloned.1.call-start = ((), (), s32[]{:S(2)}) async-start(), calls=%async_computation.4 | async-start | bytes 5308416 | tf_op jit(solution)/shard_map/all_gather | solution.py:395
  18.6 91.5 %copy-start.30 = (f32[2]{0:T(128)}, f32[2]{0:T(128)S(1)}, u32[]{:S(2)}) copy-start(f32[2]{0:T(128)S(1)} %fusion.62) | copy-start | bytes 28
  49.8 50.6 %copy-start.9 = (bf16[4,128,2048]{2,1,0:T(8,128)(2,1)S(1)}, bf16[4,128,2048]{2,1,0:T(8,128)(2,1)}, u32[]{:S(2)}) copy-start(bf16[4,128,2048]{2,1,0:T(8,128)(2,1)} %exchange.8) | copy-start | bytes 6291460
  96.2 220.1 %reduce-scatter.4.cloned.1.call-start = ((), (), s32[]{:S(2)}) async-start(), calls=%async_computation.5 | async-start | bytes 5308416 | tf_op jit(solution)/shard_map/reduce_scatter | solution.py:460
  151.2 17.0 %copy-start.2 = (bf16[128,1024]{1,0:T(8,128)(2,1)S(1)}, bf16[128,1024]{1,0:T(8,128)(2,1)}, u32[]{:S(2)}) copy-start(bf16[128,1024]{1,0:T(8,128)(2,1)} %param.20) | copy-start | bytes 786436
  169.0 55.6 %copy-start.25 = (f32[128]{0:T(128)}, f32[128]{0:T(128)S(1)}, u32[]{:S(2)}) copy-start(f32[128]{0:T(128)S(1)} %get-tuple-element.209) | copy-start | bytes 1540
  221.5 161.9 %reduce-scatter.6.cloned.1.call-start = ((), (), s32[]{:S(2)}) async-start(), calls=%async_computation.6 | async-start | bytes 1179648 | tf_op jit(solution)/shard_map/reduce_scatter | solution.py:469
  224.6 17.5 %copy-start.28 = (f32[128]{0:T(128)}, f32[128]{0:T(128)S(1)}, u32[]{:S(2)}) copy-start(f32[128]{0:T(128)S(1)} %broadcast_multiply_fusion.6) | copy-start | bytes 1540
  316.3 18.9 %copy-start.24 = (bf16[1,1,8,128]{3,1,2,0:T(2,128)(2,1)S(1)}, bf16[1,1,8,128]{3,1,2,0:T(2,128)(2,1)}, u32[]{:S(2)}) copy-start(bf16[1,1,8,128]{3,1,2,0:T(2,128)(2,1)} %copy.192) | copy-start | bytes 6148
  316.3 19.2 %copy-start.17 = (f32[1024]{0:T(1024)S(1)}, f32[1024]{0:T(1024)}, u32[]{:S(2)}) copy-start(f32[1024]{0:T(1024)} %copy-done.16) | copy-start | bytes 12292
  316.4 150.4 %reduce-scatter.8.cloned.1.call-start = ((), (), s32[]{:S(2)}) async-start(), calls=%async_computation.7 | async-start | bytes 4128768 | tf_op jit(solution)/shard_map/reduce_scatter | solution.py:538
  341.2 42.3 %copy-start.34 = (f32[2]{0:T(128)S(1)}, f32[2]{0:T(128)}, u32[]{:S(2)}) copy-start(f32[2]{0:T(128)} %get-tuple-element.175) | copy-start | bytes 28
  341.2 42.3 %copy-start.36 = (bf16[2]{0:T(256)(128)(2,1)S(1)}, bf16[2]{0:T(256)(128)(2,1)}, u32[]{:S(2)}) copy-start(bf16[2]{0:T(256)(128)(2,1)} %param.33) | copy-start | bytes 16
  341.2 42.3 %copy-start.33 = (f32[2]{0:T(128)S(1)}, f32[2]{0:T(128)}, u32[]{:S(2)}) copy-start(f32[2]{0:T(128)} %get-tuple-element.169) | copy-start | bytes 28
  384.2 8.6 %copy-start.27 = (f32[128]{0:T(128)S(1)}, f32[128]{0:T(128)}, u32[]{:S(2)}) copy-start(f32[128]{0:T(128)} %get-tuple-element.208) | copy-start | bytes 1540
  384.2 8.8 %copy-start.38 = (bf16[512,768]{1,0:T(8,128)(2,1)S(1)}, bf16[512,768]{1,0:T(8,128)(2,1)}, u32[]{:S(2)}) copy-start(bf16[512,768]{1,0:T(8,128)(2,1)} %get-tuple-element.179) | copy-start | bytes 2359300
  396.5 17.6 %copy-start.6 = (bf16[128,1024]{1,0:T(8,128)(2,1)S(1)}, bf16[128,1024]{1,0:T(8,128)(2,1)}, u32[]{:S(2)}) copy-start(bf16[128,1024]{1,0:T(8,128)(2,1)} %param.21) | copy-start | bytes 786436
  396.5 17.6 %copy-start.26 = (f32[128]{0:T(128)S(1)}, f32[128]{0:T(128)}, u32[]{:S(2)}) copy-start(f32[128]{0:T(128)} %copy-done.25) | copy-start | bytes 1540
  396.5 17.6 %copy-start.29 = (f32[128]{0:T(128)S(1)}, f32[128]{0:T(128)}, u32[]{:S(2)}) copy-start(f32[128]{0:T(128)} %copy-done.28) | copy-start | bytes 1540
  466.8 7.4 %copy-start.1 = (bf16[128,1792]{1,0:T(8,128)(2,1)S(1)}, bf16[128,1792]{1,0:T(8,128)(2,1)}, u32[]{:S(2)}) copy-start(bf16[128,1792]{1,0:T(8,128)(2,1)} %reduce-scatter.8.cloned.1.call-done) | copy-start | bytes 1376260
  (20 other events, 62.7 us)
Sparse Core Ops, SparseCore 0:
  17.4 78.7 all-gather.2
  98.2 79.1 all-gather.4
  221.6 94.6 reduce-scatter.3
  319.6 63.8 reduce-scatter.5
  386.9 79.8 reduce-scatter.7
